TPU v7x, 32 devices: a whole 2x2x4 slice. The times are simulated.
32 devices in a mesh: dp: 8 (over z, y), tensor: 4 (over x, core).
Axes of the slice: x: 2, y: 2, z: 4, core: 2. Of those that a mesh axis runs over, the one named last changes fastest.
Arguments:
- tokens: bfloat16 [8192, 512], P('dp'), may hold values from -6 to 6
- cotangent: bfloat16 [8192, 512], P('dp'), may hold values from -6 to 6
- w_query: float32 [512, 512], P('dp', 'tensor'), may hold values from -0.125 to 0.125
- w_key: float32 [512, 512], P('dp', 'tensor'), may hold values from -0.125 to 0.125
- w_value: float32 [512, 512], P('dp', 'tensor'), may hold values from -0.25 to 0.25
- w_out: float32 [512, 512], P('tensor', 'dp'), may hold values from -1 to 1
- w_gate: float32 [512, 2048], P('dp', 'tensor'), may hold values from -0.25 to 0.25
- w_up: float32 [512, 2048], P('dp', 'tensor'), may hold values from -0.25 to 0.25
- w_down: float32 [2048, 512], P('tensor', 'dp'), may hold values from -0.125 to 0.125
- norm_attn: float32 [512], P('dp'), may hold values from 0.5 to 1.5
- norm_ffn: float32 [512], P('dp'), may hold values from 0.5 to 1.5
- bias_table: float32 [32, 8], P('dp', 'tensor'), may hold values from -5 to 5
- buckets: int32 [1024, 1024], replicated, may hold values from 0 to 31
- padding: int32 [8, 1024], P('dp'), may hold values from 0 to 1, as said below
Outputs:
- block_out: bfloat16 [8192, 512], P('dp')
- input_grad: float32 [8192, 512], P('dp')
- grad_query: float32 [512, 512], P('dp', 'tensor')
- grad_key: float32 [512, 512], P('dp', 'tensor')
- grad_value: float32 [512, 512], P('dp', 'tensor')
- grad_out: float32 [512, 512], P('tensor', 'dp')
- grad_gate: float32 [512, 2048], P('dp', 'tensor')
- grad_up: float32 [512, 2048], P('dp', 'tensor')
- grad_down: float32 [2048, 512], P('tensor', 'dp')
- grad_norm_attn: float32 [512], P('dp')
- grad_norm_ffn: float32 [512], P('dp')
- grad_bias: float32 [32, 8], P('dp', 'tensor')
Inputs may be any that keep to these rules, and one draw needn't show every extreme that they name: Each row of padding is 1 on a leading run of positions, at least half of them, and 0 after it.
All inputs are finite; a program needn't handle non-finite values.
Results may differ from a plain program's by a relative error of at most 0.02.
Values may be sent and summed in bfloat16 or wider, within the bound.
A program may use at most 128 MiB of HBM per device.

v0:
```python
import jax
import jax.numpy as jnp
from jax import lax
from jax.sharding import PartitionSpec as P

epsilon = 1e-06
masked_score = -1000000000.0


def rms_scale(values, scaling):
    return values * lax.rsqrt(jnp.mean(values * values, axis=-1, keepdims=True) + epsilon) * scaling


def gated_unit(gate_proj, up_proj):
    return jax.nn.gelu(gate_proj, approximate=True) * up_proj


def dot_last(former, latter):
    return lax.dot_general(
        former, latter, (((1,), (1,)), ((), ())), preferred_element_type=jnp.float32
    )


def dot_first(former, latter):
    return lax.dot_general(
        former, latter, (((0,), (0,)), ((), ())), preferred_element_type=jnp.float32
    )


def bias_lookup(buckets, table_heads):
    bucket_ids = jnp.arange(table_heads.shape[0], dtype=jnp.int32)
    matches = buckets[None, None, :, :] == bucket_ids[:, None, None, None]
    picked = jnp.where(matches, table_heads[:, :, None, None], 0.0)
    return jnp.sum(picked, axis=0)


def bias_grad_block(grad_block, bucket_block, bucket_count):
    bucket_ids = jnp.arange(bucket_count, dtype=jnp.int32)
    matches = bucket_block[None, None, :, :] == bucket_ids[:, None, None, None]
    picked = jnp.where(matches, grad_block[None, :, :, :], 0.0)
    return jnp.sum(picked, axis=(2, 3))


def block_scores(query_block, keys_in, bias_block, padding_row):
    scores = (
        jnp.einsum("bhd,khd->hbk", query_block, keys_in, preferred_element_type=jnp.float32)
        + bias_block
    )
    return jnp.where(padding_row[None, None, :] > 0, scores, masked_score)


def attend_forward(queries, keys_in, values, padding_row, bias_blocks, block_rows):
    length, heads_here, head_size = queries.shape
    blocks = length // block_rows
    query_blocks = queries.reshape(blocks, block_rows, heads_here, head_size)

    def one_block(items):
        scores = block_scores(items[0], keys_in, items[1], padding_row)
        row_max = jnp.max(scores, axis=-1, keepdims=True)
        exponent = jnp.exp(scores - row_max)
        row_total = jnp.sum(exponent, axis=-1, keepdims=True)
        attention = (exponent / row_total).astype(jnp.bfloat16)
        head_mix = jnp.einsum("hbk,khd->bhd", attention, values, preferred_element_type=jnp.float32)
        return (head_mix.astype(jnp.bfloat16), (row_max + jnp.log(row_total))[..., 0])

    head_mix, log_totals = lax.map(one_block, (query_blocks, bias_blocks))
    return (head_mix.reshape(length, heads_here, head_size), log_totals)


def attend_backward(
    queries,
    keys_in,
    values,
    grad_mix,
    log_totals,
    padding_row,
    bias_blocks,
    bucket_blocks,
    bias_start,
    block_rows,
):
    length, heads_here, head_size = queries.shape
    blocks = length // block_rows
    bucket_count = bias_start.shape[0]
    query_blocks = queries.reshape(blocks, block_rows, heads_here, head_size)
    grad_blocks = grad_mix.reshape(blocks, block_rows, heads_here, head_size)

    def one_block(carry, items):
        grad_keys, grad_values, bias_sum = carry
        query_block, grad_block, total_block, bias_block, bucket_block = items
        scores = block_scores(query_block, keys_in, bias_block, padding_row)
        attention = jnp.exp(scores - total_block[..., None])
        grad_attention = jnp.einsum(
            "bhd,khd->hbk", grad_block, values, preferred_element_type=jnp.float32
        )
        grad_scores = attention * (
            grad_attention - jnp.sum(attention * grad_attention, axis=-1, keepdims=True)
        )
        grad_rounded = grad_scores.astype(jnp.bfloat16)
        grad_query = jnp.einsum(
            "hbk,khd->bhd", grad_rounded, keys_in, preferred_element_type=jnp.float32
        )
        grad_keys = grad_keys + jnp.einsum(
            "hbk,bhd->khd", grad_rounded, query_block, preferred_element_type=jnp.float32
        )
        grad_values = grad_values + jnp.einsum(
            "hbk,bhd->khd",
            attention.astype(jnp.bfloat16),
            grad_block,
            preferred_element_type=jnp.float32,
        )
        bias_sum = bias_sum + bias_grad_block(
            grad_rounded.astype(jnp.float32), bucket_block, bucket_count
        )
        return ((grad_keys, grad_values, bias_sum), grad_query.astype(jnp.bfloat16))

    start_carry = (
        jnp.zeros((length, heads_here, head_size), jnp.float32),
        jnp.zeros((length, heads_here, head_size), jnp.float32),
        bias_start,
    )
    (grad_keys, grad_values, bias_sum), grad_queries = lax.scan(
        one_block, start_carry, (query_blocks, grad_blocks, log_totals, bias_blocks, bucket_blocks)
    )
    return (
        grad_queries.reshape(length, heads_here, head_size),
        grad_keys.astype(jnp.bfloat16),
        grad_values.astype(jnp.bfloat16),
        bias_sum,
    )


def per_device(
    tokens,
    cotangent,
    w_query,
    w_key,
    w_value,
    w_out,
    w_gate,
    w_up,
    w_down,
    norm_attn,
    norm_ffn,
    bias_table,
    buckets,
    padding,
):
    sequences = padding.shape[0]
    length = padding.shape[1]
    block_rows = min(512, length)
    blocks = length // block_rows
    gathered = (
        lax.all_gather(w_query.astype(jnp.bfloat16), "dp", axis=0, tiled=True),
        lax.all_gather(w_key.astype(jnp.bfloat16), "dp", axis=0, tiled=True),
        lax.all_gather(w_value.astype(jnp.bfloat16), "dp", axis=0, tiled=True),
        lax.all_gather(w_gate.astype(jnp.bfloat16), "dp", axis=0, tiled=True),
        lax.all_gather(w_up.astype(jnp.bfloat16), "dp", axis=0, tiled=True),
        lax.all_gather(norm_attn.astype(jnp.bfloat16), "dp", axis=0, tiled=True),
        lax.all_gather(norm_ffn.astype(jnp.bfloat16), "dp", axis=0, tiled=True),
        lax.all_gather(bias_table.astype(jnp.bfloat16), "dp", axis=0, tiled=True),
        lax.all_gather(w_out.astype(jnp.bfloat16), "dp", axis=1, tiled=True),
        lax.all_gather(w_down.astype(jnp.bfloat16), "dp", axis=1, tiled=True),
    )
    query_full, key_full, value_full, gate_full, up_full = (
        gathered[0],
        gathered[1],
        gathered[2],
        gathered[3],
        gathered[4],
    )
    gain_attn = gathered[5].astype(jnp.float32)
    gain_ffn = gathered[6].astype(jnp.float32)
    table_heads = gathered[7].astype(jnp.float32)
    out_full, down_full = (gathered[8], gathered[9])
    heads_here = table_heads.shape[1]
    bucket_count = table_heads.shape[0]
    head_size = query_full.shape[1] // heads_here
    split_shape = (sequences, length, heads_here, head_size)
    flat_shape = (sequences * length, heads_here * head_size)
    bias_full = bias_lookup(buckets, table_heads)
    bias_blocks = jnp.transpose(
        bias_full.reshape(heads_here, blocks, block_rows, length), (1, 0, 2, 3)
    )
    bucket_blocks = buckets.reshape(blocks, block_rows, length)
    inputs = tokens.astype(jnp.float32)
    normed_low = rms_scale(inputs, gain_attn).astype(jnp.bfloat16)
    queries = jnp.dot(normed_low, query_full, preferred_element_type=jnp.float32).astype(
        jnp.bfloat16
    )
    keys_in = jnp.dot(normed_low, key_full, preferred_element_type=jnp.float32).astype(jnp.bfloat16)
    values = jnp.dot(normed_low, value_full, preferred_element_type=jnp.float32).astype(
        jnp.bfloat16
    )
    queries = queries.reshape(split_shape)
    keys_in = keys_in.reshape(split_shape)
    values = values.reshape(split_shape)

    def forward_sequence(items):
        return attend_forward(items[0], items[1], items[2], items[3], bias_blocks, block_rows)

    head_mix, log_totals = lax.map(forward_sequence, (queries, keys_in, values, padding))
    head_mix = head_mix.reshape(flat_shape)
    middle = inputs + lax.psum(
        jnp.dot(head_mix, out_full, preferred_element_type=jnp.float32), "tensor"
    )
    normed_ffn_low = rms_scale(middle, gain_ffn).astype(jnp.bfloat16)
    gate_proj = jnp.dot(normed_ffn_low, gate_full, preferred_element_type=jnp.float32)
    up_proj = jnp.dot(normed_ffn_low, up_full, preferred_element_type=jnp.float32)
    hidden = gated_unit(gate_proj, up_proj).astype(jnp.bfloat16)
    ffn_out = lax.psum(
        jnp.dot(hidden, down_full, preferred_element_type=jnp.float32).astype(jnp.bfloat16),
        "tensor",
    ).astype(jnp.float32)
    block_out = (middle + ffn_out).astype(jnp.bfloat16)
    grad_top = cotangent.astype(jnp.float32)
    grad_top_low = grad_top.astype(jnp.bfloat16)
    grad_down = dot_first(hidden, grad_top_low)
    grad_hidden = dot_last(grad_top_low, down_full)
    unit_value, unit_pull = jax.vjp(gated_unit, gate_proj, up_proj)
    grad_gate_act, grad_up_act = unit_pull(grad_hidden)
    grad_gate_low = grad_gate_act.astype(jnp.bfloat16)
    grad_up_low = grad_up_act.astype(jnp.bfloat16)
    grad_gate = dot_first(normed_ffn_low, grad_gate_low)
    grad_up = dot_first(normed_ffn_low, grad_up_low)
    partial_ffn = dot_last(grad_gate_low, gate_full) + dot_last(grad_up_low, up_full)
    grad_normed_ffn = lax.psum(partial_ffn, "tensor")
    norm_value, norm_pull = jax.vjp(rms_scale, middle, gain_ffn)
    grad_middle_norm, grad_norm_ffn = norm_pull(grad_normed_ffn)
    grad_middle = grad_top + grad_middle_norm
    grad_middle_low = grad_middle.astype(jnp.bfloat16)
    grad_out = dot_first(head_mix, grad_middle_low)
    grad_mix = dot_last(grad_middle_low, out_full).astype(jnp.bfloat16).reshape(split_shape)

    def backward_sequence(bias_carry, items):
        grad_queries, grad_keys, grad_values, bias_next = attend_backward(
            items[0],
            items[1],
            items[2],
            items[3],
            items[4],
            items[5],
            bias_blocks,
            bucket_blocks,
            bias_carry,
            block_rows,
        )
        return (bias_next, (grad_queries, grad_keys, grad_values))

    bias_start = jnp.zeros((bucket_count, heads_here), jnp.float32)
    grad_bias, (grad_queries, grad_keys, grad_values) = lax.scan(
        backward_sequence, bias_start, (queries, keys_in, values, grad_mix, log_totals, padding)
    )
    grad_queries = grad_queries.reshape(flat_shape)
    grad_keys = grad_keys.reshape(flat_shape)
    grad_values = grad_values.reshape(flat_shape)
    grad_query = dot_first(normed_low, grad_queries)
    grad_key = dot_first(normed_low, grad_keys)
    grad_value = dot_first(normed_low, grad_values)
    partial_attn = (
        dot_last(grad_queries, query_full)
        + dot_last(grad_keys, key_full)
        + dot_last(grad_values, value_full)
    )
    grad_normed_attn = lax.psum(partial_attn.astype(jnp.bfloat16), "tensor").astype(jnp.float32)
    first_value, first_pull = jax.vjp(rms_scale, inputs, gain_attn)
    grad_inputs_norm, grad_norm_attn = first_pull(grad_normed_attn)
    input_grad = grad_middle + grad_inputs_norm
    summed = (
        lax.psum_scatter(
            grad_query.astype(jnp.bfloat16), "dp", scatter_dimension=0, tiled=True
        ).astype(jnp.float32),
        lax.psum_scatter(
            grad_key.astype(jnp.bfloat16), "dp", scatter_dimension=0, tiled=True
        ).astype(jnp.float32),
        lax.psum_scatter(
            grad_value.astype(jnp.bfloat16), "dp", scatter_dimension=0, tiled=True
        ).astype(jnp.float32),
        lax.psum_scatter(
            grad_gate.astype(jnp.bfloat16), "dp", scatter_dimension=0, tiled=True
        ).astype(jnp.float32),
        lax.psum_scatter(
            grad_up.astype(jnp.bfloat16), "dp", scatter_dimension=0, tiled=True
        ).astype(jnp.float32),
        lax.psum_scatter(
            grad_norm_attn.astype(jnp.bfloat16), "dp", scatter_dimension=0, tiled=True
        ).astype(jnp.float32),
        lax.psum_scatter(
            grad_norm_ffn.astype(jnp.bfloat16), "dp", scatter_dimension=0, tiled=True
        ).astype(jnp.float32),
        lax.psum_scatter(
            grad_bias.astype(jnp.bfloat16), "dp", scatter_dimension=0, tiled=True
        ).astype(jnp.float32),
        lax.psum_scatter(
            grad_out.astype(jnp.bfloat16), "dp", scatter_dimension=1, tiled=True
        ).astype(jnp.float32),
        lax.psum_scatter(
            grad_down.astype(jnp.bfloat16), "dp", scatter_dimension=1, tiled=True
        ).astype(jnp.float32),
    )
    return (
        block_out,
        input_grad,
        summed[0],
        summed[1],
        summed[2],
        summed[8],
        summed[3],
        summed[4],
        summed[9],
        summed[5],
        summed[6],
        summed[7],
    )


def solution(mesh):
    in_specs = (
        P("dp", None),
        P("dp", None),
        P("dp", "tensor"),
        P("dp", "tensor"),
        P("dp", "tensor"),
        P("tensor", "dp"),
        P("dp", "tensor"),
        P("dp", "tensor"),
        P("tensor", "dp"),
        P("dp"),
        P("dp"),
        P("dp", "tensor"),
        P(),
        P("dp", None),
    )
    out_specs = (
        P("dp", None),
        P("dp", None),
        P("dp", "tensor"),
        P("dp", "tensor"),
        P("dp", "tensor"),
        P("tensor", "dp"),
        P("dp", "tensor"),
        P("dp", "tensor"),
        P("tensor", "dp"),
        P("dp"),
        P("dp"),
        P("dp", "tensor"),
    )
    return jax.shard_map(
        per_device, mesh=mesh, in_specs=in_specs, out_specs=out_specs, check_vma=False
    )
```

profile of v0, /device:TPU:0, one launch (start us, length us, event | category | flops | bytes accessed | tf_op | source)
XLA Modules:
  0.0 992.0 jit_solution(11852808040886161438)
XLA Ops:
  8.0 32.3 %all_gather.31 = bf16[512,128]{1,0:T(8,128)(2,1)S(1)} all-gather(bf16[64,128]{1,0:T(8,128)(2,1)S(1)} %convert_element_type.187), channel_id=1, replica_groups=mesh['dp'=8,'tensor'=4] {'dp'}, dimensions={0}, use_global_device_ids=true | all-gather | bytes 147456 | tf_op jit(solution)/shard_map/all_gather | solution.py:154
  44.1 21.4 %all-reduce.6 = (bf16[512]{0:T(512)(128)(2,1)S(1)}, bf16[512]{0:T(512)(128)(2,1)S(1)}) all-reduce(bf16[512]{0:T(512)(128)(2,1)S(1)} %dynamic-update-slice, bf16[512]{0:T(512)(128)(2,1)S(1)} %dynamic-update-slice.1), channel_id=1, replica_groups=mesh['dp'=8,'tensor'=4] {'dp'}, use_global_device_ids=true, to_apply=%add | all-reduce | flops 1024 | bytes 4096
  69.9 30.5 %all_gather.32 = bf16[512,128]{1,0:T(8,128)(2,1)S(1)} all-gather(bf16[64,128]{1,0:T(8,128)(2,1)S(1)} %convert_element_type.189), channel_id=1, replica_groups=mesh['dp'=8,'tensor'=4] {'dp'}, dimensions={0}, use_global_device_ids=true | all-gather | bytes 147456 | tf_op jit(solution)/shard_map/all_gather | solution.py:155
  101.1 16.2 %all-gather = bf16[8,4,2]{1,2,0:T(2,128)(2,1)S(1)} all-gather(bf16[1,4,2]{1,2,0:T(2,128)(2,1)S(1)} %convert_bitcast_fusion), channel_id=1, replica_groups=mesh['dp'=8,'tensor'=4] {'dp'}, dimensions={0}, use_global_device_ids=true | all-gather | bytes 144 | tf_op jit(solution)/shard_map/all_gather | solution.py:161
  117.5 22.3 %iota_compare_fusion.1 = pred[32,1024,1024]{2,1,0:T(8,128)(4,1)} fusion(s32[1024,1024]{1,0:T(8,128)} %param.30), kind=kLoop, calls=%fused_computation.49 | loop fusion | flops 33554432 | bytes 37748736 | tf_op jit(solution)/shard_map/eq | solution.py:32
  139.8 68.5 %select_reduce_fusion.1 = f32[2,1024,1024]{2,1,0:T(8,128)} fusion(f32[32,2]{1,0:T(8,128)S(1)} %bitcast.174, pred[32,1024,1024]{2,1,0:T(8,128)(4,1)} %iota_compare_fusion.1), kind=kLoop, calls=%fused_computation.48 | loop fusion | flops 132120576 | bytes 41943296 | tf_op jit(solution)/shard_map/reduce_sum | solution.py:34
  216.5 30.5 %all_gather.34 = bf16[512,128]{1,0:T(8,128)(2,1)S(1)} all-gather(bf16[64,128]{1,0:T(8,128)(2,1)S(1)} %convert_element_type.193), channel_id=1, replica_groups=mesh['dp'=8,'tensor'=4] {'dp'}, dimensions={0}, use_global_device_ids=true | all-gather | bytes 147456 | tf_op jit(solution)/shard_map/all_gather | solution.py:156
  248.5 12.4 %while.51 = (s32[]{:T(128)}, bf16[2,512,2,64]{1,3,2,0:T(8,128)(2,1)S(1)}, f32[2,2,512]{2,1,0:T(2,128)S(1)}, s32[1024]{0:T(1024)S(1)}, bf16[2,512,2,64]{1,3,2,0:T...) while((s32[]{:T(128)}, ...), condition=%wide.region_5.6_spmd, body=%wide.region_2.5_spmd.sunk | while | flops 276889600 | bytes 17603692 | solution.py:66
  261.2 30.6 %all_gather.35 = bf16[128,512]{0,1:T(8,128)(2,1)S(1)} all-gather(bf16[128,64]{0,1:T(8,128)(2,1)S(1)} %convert_element_type.195), channel_id=1, replica_groups=mesh['dp'=8,'tensor'=4] {'dp'}, dimensions={1}, use_global_device_ids=true | all-gather | bytes 147456 | tf_op jit(solution)/shard_map/all_gather | solution.py:162
  293.8 31.5 %all_gather.37 = bf16[512,512]{1,0:T(8,128)(2,1)S(1)} all-gather(bf16[64,512]{1,0:T(8,128)(2,1)S(1)} %convert_element_type.199), channel_id=1, replica_groups=mesh['dp'=8,'tensor'=4] {'dp'}, dimensions={0}, use_global_device_ids=true | all-gather | bytes 589824 | tf_op jit(solution)/shard_map/all_gather | solution.py:157
  325.3 33.3 %all_gather.38 = bf16[512,512]{1,0:T(8,128)(2,1)} all-gather(bf16[64,512]{1,0:T(8,128)(2,1)S(1)} %convert_element_type.200), channel_id=1, replica_groups=mesh['dp'=8,'tensor'=4] {'dp'}, dimensions={0}, use_global_device_ids=true | all-gather | bytes 589824 | tf_op jit(solution)/shard_map/all_gather | solution.py:158
  358.6 33.3 %all_gather.39 = bf16[512,512]{0,1:T(8,128)(2,1)} all-gather(bf16[512,64]{0,1:T(8,128)(2,1)S(1)} %convert_element_type.202), channel_id=1, replica_groups=mesh['dp'=8,'tensor'=4] {'dp'}, dimensions={1}, use_global_device_ids=true | all-gather | bytes 589824 | tf_op jit(solution)/shard_map/all_gather | solution.py:163
  415.3 38.6 %all-reduce.14.cloned.1.call-done = f32[1024,512]{1,0:T(8,128)} async-done(((f32[1024,512]{1,0:T(8,128)}), f32[1024,512]{1,0:T(8,128)}) %all-reduce.14.cloned.1.call-update) | async-done | bytes 2097168 | tf_op jit(solution)/shard_map/psum | solution.py:227
  460.6 97.7 %while.52 = (s32[]{:T(128)}, f32[1024,2,64]{0,2,1:T(8,128)}, f32[1024,2,64]{0,2,1:T(8,128)S(1)}, f32[32,2]{1,0:T(8,128)S(1)}, bf16[2,512,2,64]{1,3,2,0:T(8,128)(...) while((s32[]{:T(128)}, f32[1024,2,64]{0,2,1:T(8,128)}, ...), condition=%wide.region_14.15_spmd.clone, body=%wide.region_11.14_spmd.clone.sunk | while | flops 766050368 | bytes 123105576 | solution.py:122
  474.1 10.0 %iota_compare_fusion.3 = pred[32,512,1024]{2,1,0:T(8,128)(4,1)S(1)} fusion(s32[512,1024]{1,0:T(8,128)S(1)} %dynamic-slice_bitcast_fusion.5), kind=kLoop, calls=%fused_computation.15.clone.1 | loop fusion | flops 16777216 | bytes 18874368 | tf_op jit(solution)/shard_map/while/body/eval_jaxpr/while/body/eval_jaxpr/eq | solution.py:39
  484.1 23.3 %select_reduce_fusion.3 = f32[32,2]{1,0:T(8,128)S(1)} fusion(f32[2,512,1024]{2,1,0:T(8,128)} %get-tuple-element.550, pred[32,512,1024]{2,1,0:T(8,128)(4,1)S(1)} %iota_compare_fusion.3), kind=kLoop, calls=%fused_computation.14.clone.1 | loop fusion | flops 67108800 | bytes 20971776 | tf_op jit(solution)/shard_map/while/body/eval_jaxpr/while/body/eval_jaxpr/reduce_sum | solution.py:41
  533.5 23.3 %select_reduce_fusion.3 = f32[32,2]{1,0:T(8,128)S(1)} fusion(f32[2,512,1024]{2,1,0:T(8,128)} %get-tuple-element.550, pred[32,512,1024]{2,1,0:T(8,128)(4,1)S(1)} %iota_compare_fusion.3), kind=kLoop, calls=%fused_computation.14.clone.1 | loop fusion | flops 67108800 | bytes 20971776 | tf_op jit(solution)/shard_map/while/body/eval_jaxpr/while/body/eval_jaxpr/reduce_sum | solution.py:41
  585.3 62.7 %reduce-scatter.21.cloned.1.call-done = bf16[512,64]{0,1:T(8,128)(2,1)} async-done(((bf16[512,512]{0,1:T(8,128)(2,1)}), bf16[512,64]{0,1:T(8,128)(2,1)}) %reduce-scatter.21.cloned.1.call-update) | async-done | bytes 65552 | tf_op jit(solution)/shard_map/reduce_scatter | solution.py:297
  649.5 61.9 %reduce-scatter.9.cloned.1.call-done = bf16[64,128]{1,0:T(8,128)(2,1)} async-done(((bf16[512,128]{1,0:T(8,128)(2,1)}), bf16[64,128]{1,0:T(8,128)(2,1)}) %reduce-scatter.9.cloned.1.call-update) | async-done | bytes 16400 | tf_op jit(solution)/shard_map/reduce_scatter | solution.py:270
  712.8 62.3 %reduce-scatter.11.cloned.1.call-done = bf16[64,128]{1,0:T(8,128)(2,1)} async-done(((bf16[512,128]{1,0:T(8,128)(2,1)}), bf16[64,128]{1,0:T(8,128)(2,1)}) %reduce-scatter.11.cloned.1.call-update) | async-done | bytes 16400 | tf_op jit(solution)/shard_map/reduce_scatter | solution.py:273
  776.4 62.2 %reduce-scatter.13.cloned.1.call-done = bf16[64,128]{1,0:T(8,128)(2,1)} async-done(((bf16[512,128]{1,0:T(8,128)(2,1)}), bf16[64,128]{1,0:T(8,128)(2,1)}) %reduce-scatter.13.cloned.1.call-update) | async-done | bytes 16400 | tf_op jit(solution)/shard_map/reduce_scatter | solution.py:276
  839.9 62.3 %reduce-scatter.15.cloned.1.call-done = bf16[128,64]{0,1:T(8,128)(2,1)} async-done(((bf16[128,512]{0,1:T(8,128)(2,1)}), bf16[128,64]{0,1:T(8,128)(2,1)}) %reduce-scatter.15.cloned.1.call-update) | async-done | bytes 16400 | tf_op jit(solution)/shard_map/reduce_scatter | solution.py:294
  903.6 52.3 %all-reduce.16.cloned.1.call-done = (bf16[1024,512]{1,0:T(8,128)(2,1)}, bf16[1024,512]{1,0:T(8,128)(2,1)}) async-done(((bf16[1024,512]{1,0:T(8,128)(2,1)}, bf16[1024,512]{1,0:T(8,128)(2,1)}), (bf16[1024,512]{1,0:T(8,128)(2,1)}, bf16[1024,512]{1,0:T(8,128)(2,1)})) %all-reduce.16.cloned.1.call-update) | async-done | bytes 2097168 | tf_op jit(solution)/shard_map/psum | solution.py:211
  962.6 21.4 %all-reduce.5 = (bf16[512]{0:T(512)(128)(2,1)S(1)}, bf16[512]{0:T(512)(128)(2,1)S(1)}, bf16[32,2]{0,1:T(2,128)(2,1)S(1)}) all-reduce(bf16[512]{0:T(512)(128)(2,1)S(1)} %get-tuple-element.343, bf16[512]{0:T(512)(128)(2,1)S(1)} %copy-done.51, bf16[32,2]{0,1:T(2,128)(2,1)S(1)} %copy.77), channel_id=9, replica_groups=mesh['dp'=8,'tensor'=4] {'dp'}, use_global_device_ids=true, to_apply=%region_25.26.clone | all-reduce | flops 1088 | bytes 4352
  (248 shorter events, 144.3 us)
Async XLA Ops:
  7.2 384.8 %all-reduce.12.cloned.1.call-start = ((), (), s32[]{:S(2)}) async-start(), calls=%async_computation.7 | async-start | bytes 4194304 | tf_op jit(solution)/shard_map/psum | solution.py:204
  65.4 181.6 %copy-start.47 = (f32[512]{0:T(512)}, f32[512]{0:T(512)S(1)}, u32[]{:S(2)}) copy-start(f32[512]{0:T(512)S(1)} %convert_element_type.185) | copy-start | bytes 6148
  67.0 33.5 %copy-start.8 = (bf16[1024,512]{1,0:T(8,128)(2,1)S(1)}, bf16[1024,512]{1,0:T(8,128)(2,1)}, u32[]{:S(2)}) copy-start(bf16[1024,512]{1,0:T(8,128)(2,1)} %param.18) | copy-start | bytes 3145732
  67.5 179.5 %copy-start.38 = (f32[1024]{0:T(1024)}, f32[1024]{0:T(1024)S(1)}, u32[]{:S(2)}) copy-start(f32[1024]{0:T(1024)S(1)} %fusion.53) | copy-start | bytes 12292
  69.3 31.8 %copy-start.52 = (f32[4,2]{0,1:T(2,128)S(1)}, f32[4,2]{0,1:T(2,128)}, u32[]{:S(2)}) copy-start(f32[4,2]{0,1:T(2,128)} %param.29) | copy-start | bytes 100
  100.5 39.3 %copy-start.29 = (bf16[512,128]{1,0:T(8,128)(2,1)}, bf16[512,128]{1,0:T(8,128)(2,1)S(1)}, u32[]{:S(2)}) copy-start(bf16[512,128]{1,0:T(8,128)(2,1)S(1)} %all_gather.32) | copy-start | bytes 393220
  216.5 31.9 %copy-start.34 = (s32[1,1024]{1,0:T(1,128)S(1)}, s32[1,1024]{1,0:T(1,128)}, u32[]{:S(2)}) copy-start(s32[1,1024]{1,0:T(1,128)} %param.31) | copy-start | bytes 12292
  293.6 160.3 %all-reduce.14.cloned.1.call-start = ((), (), s32[]{:S(2)}) async-start(), calls=%async_computation.8 | async-start | bytes 4194304 | tf_op jit(solution)/shard_map/psum | solution.py:227
  394.1 62.7 %copy-start.1 = (f32[1024,512]{1,0:T(8,128)}, f32[1024,512]{1,0:T(8,128)S(1)}, u32[]{:S(2)}) copy-start(f32[1024,512]{1,0:T(8,128)S(1)} %get-tuple-element.397) | copy-start | bytes 6291460
  403.6 174.4 %reduce-scatter.17.cloned.1.call-start = ((), (), s32[]{:S(2)}) async-start(), calls=%async_computation.13 | async-start | bytes 589824 | tf_op jit(solution)/shard_map/reduce_scatter | solution.py:279
  406.8 177.0 %reduce-scatter.19.cloned.1.call-start = ((), (), s32[]{:S(2)}) async-start(), calls=%async_computation.14 | async-start | bytes 589824 | tf_op jit(solution)/shard_map/reduce_scatter | solution.py:282
  410.3 237.7 %reduce-scatter.21.cloned.1.call-start = ((), (), s32[]{:S(2)}) async-start(), calls=%async_computation.15 | async-start | bytes 589824 | tf_op jit(solution)/shard_map/reduce_scatter | solution.py:297
  415.2 296.2 %reduce-scatter.9.cloned.1.call-start = ((), (), s32[]{:S(2)}) async-start(), calls=%async_computation.9 | async-start | bytes 147456 | tf_op jit(solution)/shard_map/reduce_scatter | solution.py:270
  460.6 99.8 %copy-start.39 = (f32[1024]{0:T(1024)S(1)}, f32[1024]{0:T(1024)}, u32[]{:S(2)}) copy-start(f32[1024]{0:T(1024)} %copy-done.38) | copy-start | bytes 12292
  460.6 99.8 %copy-start.48 = (f32[512]{0:T(512)S(1)}, f32[512]{0:T(512)}, u32[]{:S(2)}) copy-start(f32[512]{0:T(512)} %copy-done.47) | copy-start | bytes 6148
  563.1 212.0 %reduce-scatter.11.cloned.1.call-start = ((), (), s32[]{:S(2)}) async-start(), calls=%async_computation.10 | async-start | bytes 147456 | tf_op jit(solution)/shard_map/reduce_scatter | solution.py:273
  567.1 271.6 %reduce-scatter.13.cloned.1.call-start = ((), (), s32[]{:S(2)}) async-start(), calls=%async_computation.11 | async-start | bytes 147456 | tf_op jit(solution)/shard_map/reduce_scatter | solution.py:276
  571.1 331.1 %reduce-scatter.15.cloned.1.call-start = ((), (), s32[]{:S(2)}) async-start(), calls=%async_computation.12 | async-start | bytes 147456 | tf_op jit(solution)/shard_map/reduce_scatter | solution.py:294
  573.0 382.9 %all-reduce.16.cloned.1.call-start = ((), (), s32[]{:S(2)}) async-start(), calls=%async_computation.16 | async-start | bytes 4194304 | tf_op jit(solution)/shard_map/psum | solution.py:211
  573.3 382.6 %copy-start.10 = (bf16[1024,512]{1,0:T(8,128)(2,1)S(1)}, bf16[1024,512]{1,0:T(8,128)(2,1)}, u32[]{:S(2)}) copy-start(bf16[1024,512]{1,0:T(8,128)(2,1)} %param.18) | copy-start | bytes 3145732
  576.5 379.4 %copy-start.41 = (f32[1024]{0:T(1024)S(1)}, f32[1024]{0:T(1024)}, u32[]{:S(2)}) copy-start(f32[1024]{0:T(1024)} %copy-done.38) | copy-start | bytes 12292
  576.5 379.4 %copy-start.50 = (f32[512]{0:T(512)S(1)}, f32[512]{0:T(512)}, u32[]{:S(2)}) copy-start(f32[512]{0:T(512)} %copy-done.47) | copy-start | bytes 6148
  576.5 381.9 %copy-start.43 = (f32[1024]{0:T(1024)S(1)}, f32[1024]{0:T(1024)}, u32[]{:S(2)}) copy-start(f32[1024]{0:T(1024)} %copy-done.42) | copy-start | bytes 12292
  576.5 381.9 %copy-start.2 = (f32[1024,512]{1,0:T(8,128)S(1)}, f32[1024,512]{1,0:T(8,128)}, u32[]{:S(2)}) copy-start(f32[1024,512]{1,0:T(8,128)} %copy-done.1) | copy-start | bytes 6291460
  (44 other events, 215.1 us)
Sparse Core Ops, SparseCore 0:
  293.8 50.1 all-reduce.11
  403.8 50.0 all-reduce.13
  457.3 62.0 reduce-scatter.16
  522.9 60.8 reduce-scatter.18
  587.0 60.9 reduce-scatter.20
  651.5 59.8 reduce-scatter.8
  715.1 59.8 reduce-scatter.10
  778.7 59.8 reduce-scatter.12
  842.3 59.8 reduce-scatter.14
  905.2 50.5 all-reduce.15
where the time goes:
time: 993 us; the launch traced here: 992 us
  waiting for transfers between devices  407 us (41%)
  blocking collectives  281 us (28%)
  other arithmetic  193 us (19%)
  matrix products  70.6 us (7%)
  local copies, waits for them, and re-layouts  23.4 us (2%)
  between operations  16.9 us (2%)
    reduce_sum x1, other arithmetic, bias_lookup(): return jnp.sum(picked, axis=0)  68.5 us
    reduce_scatter x1, waiting for transfers between devices, per_device(): lax.psum_scatter(grad_down.astype(jnp.bfloat16), 'dp', scatter_dimension=...  62.7 us
    reduce_scatter x1, waiting for transfers between devices, per_device(): lax.psum_scatter(grad_out.astype(jnp.bfloat16), 'dp', scatter_dimension=1...  62.3 us
    reduce_scatter x1, waiting for transfers between devices, per_device(): lax.psum_scatter(grad_key.astype(jnp.bfloat16), 'dp', scatter_dimension=0...  62.3 us
    reduce_scatter x1, waiting for transfers between devices, per_device(): lax.psum_scatter(grad_value.astype(jnp.bfloat16), 'dp', scatter_dimension...  62.2 us
    reduce_scatter x1, waiting for transfers between devices, per_device(): lax.psum_scatter(grad_query.astype(jnp.bfloat16), 'dp', scatter_dimension...  61.9 us
    psum x1, waiting for transfers between devices, per_device(): lax.psum(jnp.dot(hidden, down_full, preferred_element_type=jnp.float32).a...  52.3 us
    reduce_sum x2, other arithmetic, bias_grad_block(): return jnp.sum(picked, axis=(2, 3))  46.6 us
  transfers between devices with their start and end apart: 10, of which 8 were waited for; matrix products, arithmetic and copies ran while one was open for 14% of the time, Pallas kernels for 0%

commit v1 on v0

v1 whole, which is shorter than its diff:
```python
import functools

import jax
import jax.numpy as jnp
from jax import lax
from jax.experimental import pallas as pl
from jax.experimental.pallas import tpu as pltpu
from jax.sharding import PartitionSpec as P

MESH = pl.DeviceIdType.MESH
BF = jnp.bfloat16
F32 = jnp.float32
NN = (((1,), (0,)), ((), ()))
NT = (((1,), (1,)), ((), ()))
TN = (((0,), (0,)), ((), ()))
epsilon = 1e-06
masked_score = -1000000000.0
LANES = 128
BUCKETS = 32


def dot(former, latter, dims):
    return lax.dot_general(former, latter, dims, preferred_element_type=F32)


def rows_of(index, size):
    return pl.ds(pl.multiple_of(index * size, size), size)


def lookup(table, ids):
    tiles = ids.shape[1] // LANES
    return jnp.concatenate(
        [
            jnp.take_along_axis(table, ids[:, c * LANES : (c + 1) * LANES], axis=1)
            for c in range(tiles)
        ],
        axis=1,
    )


class Comm:
    def __init__(self, sizes, sems):
        self.Z, self.Y, self.X = sizes
        self.sems = sems
        self.used = 0
        self.d, self.t = lax.axis_index("dp"), lax.axis_index("tensor")
        self.z, self.y = self.d // self.Y, self.d % self.Y
        self.x, self.c = self.t // 2, self.t % 2
        self.pending = []

    def z_peer(self, k):
        return ((self.z + k) % self.Z) * self.Y + self.y, self.t

    def y_peer(self, j):
        return self.z * self.Y + (self.y + j) % self.Y, self.t

    def x_peer(self, j):
        return self.d, ((self.x + j) % self.X) * 2 + self.c

    def core_peer(self):
        return self.d, self.x * 2 + (1 - self.c)

    def origin(self, kz, j=0):
        return ((self.z - kz) % self.Z) * self.Y + (self.y - j) % self.Y

    def pair(self):
        self.used += 2
        return self.sems.at[self.used - 2], self.sems.at[self.used - 1]

    def barrier(self):
        peers = [self.z_peer(k) for k in range(1, self.Z)]
        peers += [self.y_peer(j) for j in range(1, self.Y)]
        peers += [self.x_peer(j) for j in range(1, self.X)]
        peers += [self.core_peer()]
        semaphore = pltpu.get_barrier_semaphore()
        for peer in peers:
            pl.semaphore_signal(semaphore, inc=1, device_id=peer, device_id_type=MESH)
        pl.semaphore_wait(semaphore, len(peers))

    def copy(self, src, dst, peer, pair):
        return pltpu.make_async_remote_copy(
            src_ref=src,
            dst_ref=dst,
            send_sem=pair[0],
            recv_sem=pair[1],
            device_id=peer,
            device_id_type=MESH,
        )

    def send(self, src, dst, peer, pair):
        made = self.copy(src, dst, peer, pair)
        made.start()
        self.pending.append(made)

    def drain(self):
        for made in self.pending:
            made.wait_send()
        self.pending = []


class Gather:
    def __init__(self, comm, full):
        self.comm, self.full = comm, full
        Z, Y = comm.Z, comm.Y
        self.zp = {k: comm.pair() for k in range(1, Z)}
        self.yp = {(k, j): comm.pair() for k in range(Z) for j in range(1, Y)}

    def send_y(self, k):
        m = self.comm
        block = self.full.at[m.origin(k)]
        for j in range(1, m.Y):
            m.send(block, block, m.y_peer(j), self.yp[k, j])

    def start(self):
        m = self.comm
        own = self.full.at[m.d]
        for k in range(m.Z - 1, 0, -1):
            m.send(own, own, m.z_peer(k), self.zp[k])
        self.send_y(0)

    def forward(self):
        m = self.comm
        for k in range(1, m.Z):
            block = self.full.at[m.origin(k)]
            m.copy(block, block, m.z_peer(k), self.zp[k]).wait_recv()
            self.send_y(k)

    def finish(self):
        m = self.comm
        for k in range(m.Z):
            for j in range(1, m.Y):
                block = self.full.at[m.origin(k, j)]
                m.copy(block, block, m.y_peer(j), self.yp[k, j]).wait_recv()


def first_kernel(
    sizes,
    heads,
    x_hbm,
    wq_hbm,
    wk_hbm,
    wv_hbm,
    wo_hbm,
    wg_hbm,
    wu_hbm,
    wd_hbm,
    ga_hbm,
    gf_hbm,
    bt_hbm,
    bucket_hbm,
    pad_hbm,
    wa_out,
    wo_out,
    wg_out,
    wu_out,
    wd_out,
    misc_out,
    n1_out,
    q_out,
    k_out,
    v_out,
    p_out,
    o_out,
    x_v,
    sa,
    so,
    sg,
    su,
    sd,
    sga,
    sgf,
    sbt,
    bucket_v,
    pad_v,
    wa,
    wo,
    wg,
    wu,
    wd,
    misc,
    n1_v,
    q_v,
    k_v,
    v_v,
    p_v,
    o_v,
    local_sems,
    out_sems,
    sems,
):
    T, D = x_v.shape
    dp, R, I3 = wa.shape
    BR, _ = bt_hbm.shape
    I = wo.shape[2]
    HD = I // heads
    loads = [
        (wq_hbm, sa.at[0]),
        (wk_hbm, sa.at[1]),
        (wv_hbm, sa.at[2]),
        (ga_hbm, sga),
        (gf_hbm, sgf),
        (bt_hbm, sbt),
        (wo_hbm, so),
        (wg_hbm, sg),
        (wu_hbm, su),
        (wd_hbm, sd),
        (x_hbm, x_v),
        (bucket_hbm, bucket_v),
        (pad_hbm, pad_v),
    ]
    loads = [pltpu.make_async_copy(a, b, local_sems.at[n]) for n, (a, b) in enumerate(loads)]
    for load in loads:
        load.start()
    comm = Comm(sizes, sems)
    comm.barrier()
    g_misc, g_a, g_o, g_g, g_u, g_d = [Gather(comm, f) for f in (misc, wa, wo, wg, wu, wd)]
    d = comm.d
    for load in loads[:6]:
        load.wait()
    for n in range(3):
        wa[d, :, n * I : (n + 1) * I] = sa[n].astype(BF)
    misc[d] = jnp.zeros(misc.shape[1:], F32)
    misc[d, 0:1, 0:R] = sga[...]
    misc[d, 1:2, 0:R] = sgf[...]
    misc[d, 2 : 2 + BR, 0:heads] = sbt[...]
    g_a.start()
    g_misc.start()
    loads[6].wait()
    wo[d] = so[...].T.astype(BF)
    g_o.start()
    loads[7].wait()
    wg[d] = sg[...].astype(BF)
    g_g.start()
    loads[8].wait()
    wu[d] = su[...].astype(BF)
    g_u.start()
    loads[9].wait()
    wd[d] = sd[...].T.astype(BF)
    g_d.start()
    for load in loads[10:]:
        load.wait()
    g_a.forward()
    g_misc.forward()
    g_a.finish()
    g_misc.finish()
    gain = jnp.concatenate([misc[n, 0:1, 0:R] for n in range(dp)], axis=1)
    gain = gain.astype(BF).astype(F32)
    flat = misc[...].reshape(dp * 8, LANES).astype(BF)
    row = lax.broadcasted_iota(jnp.int32, flat.shape, 0)
    lane = lax.broadcasted_iota(jnp.int32, flat.shape, 1)
    chosen = (row // 8 == lane // BR) & (row % 8 - 2 == lane % BR) & (lane < BUCKETS)
    table = dot(flat, jnp.where(chosen, 1.0, 0.0).astype(BF), TN)[0:8]
    block = 256

    def project(i, carry):
        rows = rows_of(i, block)
        x = x_v[rows, :].astype(F32)
        r = lax.rsqrt(jnp.mean(x * x, axis=1, keepdims=True) + epsilon)
        n1 = (x * r * gain).astype(BF)
        n1_v[rows, :] = n1
        made = dot(n1, wa[...].reshape(D, I3), NN).astype(BF)
        for h in range(heads):
            for n, ref in enumerate((q_v, k_v, v_v)):
                ref[h, rows, :] = made[:, n * I + h * HD : n * I + (h + 1) * HD]
        return carry

    lax.fori_loop(0, T // block, project, 0)
    g_o.forward()
    g_g.forward()
    real = pad_v[...] > 0
    sub = 128

    def attend(i, carry):
        rows = rows_of(i, sub)
        ids = bucket_v[rows, :]
        for h in range(heads):
            scores = dot(q_v[h, rows, :], k_v[h], NT)
            bias = lookup(jnp.broadcast_to(table[h : h + 1, :], (sub, LANES)), ids)
            scores = jnp.where(real, scores + bias, masked_score)
            top = jnp.max(scores, axis=1, keepdims=True)
            e = jnp.exp(scores - top)
            inverse = 1.0 / jnp.sum(e, axis=1, keepdims=True)
            p = (e * inverse).astype(BF)
            p_v[h, rows, :] = p
            o_v[h, rows, :] = dot(p, v_v[h], NN)
        return carry

    lax.fori_loop(0, T // sub, attend, 0)
    g_u.forward()
    g_d.forward()
    for g in (g_o, g_g, g_u, g_d):
        g.finish()
    comm.drain()
    stores = [
        (wa, wa_out),
        (wo, wo_out),
        (wg, wg_out),
        (wu, wu_out),
        (wd, wd_out),
        (misc, misc_out),
        (n1_v, n1_out),
        (q_v, q_out),
        (k_v, k_out),
        (v_v, v_out),
        (p_v, p_out),
        (o_v, o_out),
    ]
    stores = [pltpu.make_async_copy(a, b, out_sems.at[n]) for n, (a, b) in enumerate(stores)]
    for store in stores:
        store.start()
    for store in stores:
        store.wait()


def back_kernel(heads, q_v, k_v, v_v, do_v, o_v, p_v, bucket_v, dq_o, dk_o, dv_o, bg_o, ds_v):
    T = q_v.shape[1]
    G = 32
    sub = 128
    bg_o[...] = jnp.zeros_like(bg_o)

    def body(i, carry):
        rows = rows_of(i, sub)
        kept = []
        for h in range(heads):
            do = do_v[h, rows, :]
            delta = jnp.sum(do.astype(F32) * o_v[h, rows, :], axis=1, keepdims=True)
            dp = dot(do, v_v[h], NT)
            ds = (p_v[h, rows, :].astype(F32) * (dp - delta)).astype(BF)
            ds_v[h, rows, :] = ds
            kept.append(ds)
            dq_o[h, rows, :] = dot(ds, k_v[h], NN).astype(BF)
        ids = bucket_v[rows, :]
        high = (ids >> 2).astype(BF)
        low = (ids & 3).astype(BF)
        for g in range(sub // G):
            part = slice(g * G, (g + 1) * G)
            hi, lo = high[part], low[part]
            one, zero = jnp.ones_like(hi), jnp.zeros_like(hi)
            left = jnp.concatenate(
                [jnp.where(hi == BF(b), one, zero) for b in range(BUCKETS // 4)], axis=0
            )
            right = []
            for b in range(4):
                match = lo == BF(b)
                right += [jnp.where(match, ds[part], zero) for ds in kept]
            bg_o[...] += dot(left, jnp.concatenate(right, axis=0), NT)
        return carry

    lax.fori_loop(0, T // sub, body, 0)
    for h in range(heads):
        dk_o[h] = dot(ds_v[h], q_v[h], TN).astype(BF)
        dv_o[h] = dot(p_v[h], do_v[h], TN).astype(BF)
    left = lax.broadcasted_iota(jnp.int32, bg_o.shape, 0)
    right = lax.broadcasted_iota(jnp.int32, bg_o.shape, 1)
    bg_o[...] = jnp.where(left % G == right % G, bg_o[...], 0.0)


def rms_scale(values, scaling):
    return values * lax.rsqrt(jnp.mean(values * values, axis=-1, keepdims=True) + epsilon) * scaling


def gated_unit(gate_proj, up_proj):
    return jax.nn.gelu(gate_proj, approximate=True) * up_proj


def per_device(
    sizes,
    tokens,
    cotangent,
    w_query,
    w_key,
    w_value,
    w_out,
    w_gate,
    w_up,
    w_down,
    norm_attn,
    norm_ffn,
    bias_table,
    buckets,
    padding,
):
    T, D = tokens.shape
    R, I = w_query.shape
    F = w_gate.shape[1]
    BR, heads = bias_table.shape
    HD = I // heads
    Z, Y, X = sizes
    dp = Z * Y
    S = jax.ShapeDtypeStruct
    V = pltpu.VMEM
    shapes = [
        S((dp, R, 3 * I), BF),
        S((dp, R, I), BF),
        S((dp, R, F), BF),
        S((dp, R, F), BF),
        S((dp, R, F), BF),
        S((dp, 8, LANES), F32),
        S((T, D), BF),
        S((heads, T, HD), BF),
        S((heads, T, HD), BF),
        S((heads, T, HD), BF),
        S((heads, T, T), BF),
        S((heads, T, HD), F32),
    ]
    wa, wo, wg, wu, wd, misc, normed_low, q, k, v, p, o = pl.pallas_call(
        functools.partial(first_kernel, sizes, heads),
        out_shape=shapes,
        in_specs=[pl.BlockSpec(memory_space=pl.ANY)] * 13,
        out_specs=[pl.BlockSpec(memory_space=pl.ANY)] * len(shapes),
        scratch_shapes=[
            V((T, D), BF),
            V((3, R, I), F32),
            V((I, R), F32),
            V((R, F), F32),
            V((R, F), F32),
            V((F, R), F32),
            V((1, R), F32),
            V((1, R), F32),
            V((BR, heads), F32),
            V((T, T), jnp.int32),
            V((1, T), jnp.int32),
        ]
        + [V(s.shape, s.dtype) for s in shapes]
        + [
            pltpu.SemaphoreType.DMA((13,)),
            pltpu.SemaphoreType.DMA((12,)),
            pltpu.SemaphoreType.DMA((12 * (Z - 1 + Z * (Y - 1)),)),
        ],
        compiler_params=pltpu.CompilerParams(
            collective_id=0, has_side_effects=True, vmem_limit_bytes=60 << 20
        ),
        name="gather_attend",
    )(
        tokens,
        w_query,
        w_key,
        w_value,
        w_out,
        w_gate,
        w_up,
        w_down,
        norm_attn.reshape(1, R),
        norm_ffn.reshape(1, R),
        bias_table,
        buckets,
        padding,
    )
    wa = wa.reshape(D, 3 * I)
    query_full, key_full, value_full = wa[:, :I], wa[:, I : 2 * I], wa[:, 2 * I :]
    out_t, gate_full, up_full, down_t = [w.reshape(D, -1) for w in (wo, wg, wu, wd)]
    gain_attn = misc[:, 0, :R].reshape(D).astype(BF).astype(F32)
    gain_ffn = misc[:, 1, :R].reshape(D).astype(BF).astype(F32)
    inputs = tokens.astype(F32)
    head_mix = jnp.transpose(o, (1, 0, 2)).reshape(T, I).astype(BF)
    middle = inputs + lax.psum(dot(head_mix, out_t, NT), "tensor")
    normed_ffn_low = rms_scale(middle, gain_ffn).astype(BF)
    gate_proj = dot(normed_ffn_low, gate_full, NN)
    up_proj = dot(normed_ffn_low, up_full, NN)
    hidden = gated_unit(gate_proj, up_proj).astype(BF)
    ffn_out = lax.psum(dot(hidden, down_t, NT).astype(BF), "tensor").astype(F32)
    block_out = (middle + ffn_out).astype(BF)
    grad_top = cotangent.astype(F32)
    grad_down = dot(cotangent, hidden, TN)
    grad_hidden = dot(cotangent, down_t, NN)
    _, unit_pull = jax.vjp(gated_unit, gate_proj, up_proj)
    grad_gate_act, grad_up_act = unit_pull(grad_hidden)
    grad_gate_low = grad_gate_act.astype(BF)
    grad_up_low = grad_up_act.astype(BF)
    grad_gate = dot(normed_ffn_low, grad_gate_low, TN)
    grad_up = dot(normed_ffn_low, grad_up_low, TN)
    partial_ffn = dot(grad_gate_low, gate_full, NT) + dot(grad_up_low, up_full, NT)
    grad_normed_ffn = lax.psum(partial_ffn, "tensor")
    _, norm_pull = jax.vjp(rms_scale, middle, gain_ffn)
    grad_middle_norm, grad_norm_ffn = norm_pull(grad_normed_ffn)
    grad_middle = grad_top + grad_middle_norm
    grad_middle_low = grad_middle.astype(BF)
    grad_out = dot(grad_middle_low, head_mix, TN)
    grad_mix = dot(grad_middle_low, out_t, NN).astype(BF)
    do = jnp.transpose(grad_mix.reshape(T, heads, HD), (1, 0, 2))
    VM = pl.BlockSpec(memory_space=pltpu.VMEM)
    wide = 32 * 4 * heads
    dq, dk, dv, bg = pl.pallas_call(
        functools.partial(back_kernel, heads),
        out_shape=[
            S((heads, T, HD), BF),
            S((heads, T, HD), BF),
            S((heads, T, HD), BF),
            S((256, wide), F32),
        ],
        in_specs=[VM] * 7,
        out_specs=[VM] * 4,
        scratch_shapes=[V((heads, T, T), BF)],
        compiler_params=pltpu.CompilerParams(vmem_limit_bytes=60 << 20),
        name="attend_back",
    )(q, k, v, do, o, p, buckets)
    grad_bias = jnp.sum(bg.reshape(8, 32, 4, heads, 32), axis=(1, 4)).reshape(BUCKETS, heads)
    flat = lambda a: jnp.transpose(a, (1, 0, 2)).reshape(T, I)
    dq, dk, dv = flat(dq), flat(dk), flat(dv)
    partial_attn = dot(dq, query_full, NT) + dot(dk, key_full, NT) + dot(dv, value_full, NT)
    grad_normed_attn = lax.psum(partial_attn.astype(BF), "tensor").astype(F32)
    _, first_pull = jax.vjp(rms_scale, inputs, gain_attn)
    grad_inputs_norm, grad_norm_attn = first_pull(grad_normed_attn)
    input_grad = grad_middle + grad_inputs_norm
    packed = jnp.concatenate(
        [dot(normed_low, a, TN).astype(BF) for a in (dq, dk, dv)]
        + [a.astype(BF) for a in (grad_out, grad_gate, grad_up, grad_down)],
        axis=1,
    )
    summed = lax.psum_scatter(packed, "dp", scatter_dimension=0, tiled=True).astype(F32)
    cuts = [0, I, 2 * I, 3 * I, 4 * I, 4 * I + F, 4 * I + 2 * F, 4 * I + 3 * F]
    g_q, g_k, g_v, g_o, g_g, g_u, g_d = [summed[:, a:b] for a, b in zip(cuts, cuts[1:])]
    scatter = lambda a: lax.psum_scatter(
        a.astype(BF), "dp", scatter_dimension=0, tiled=True
    ).astype(F32)
    return (
        block_out,
        input_grad,
        g_q,
        g_k,
        g_v,
        g_o.T,
        g_g,
        g_u,
        g_d.T,
        scatter(grad_norm_attn),
        scatter(grad_norm_ffn),
        scatter(grad_bias),
    )


def solution(mesh):
    shards, halves = mesh.shape["dp"], mesh.shape["tensor"]
    X = halves // 2
    Y = X if shards % X == 0 else 1
    sizes = (shards // Y, Y, X)
    in_specs = (
        P("dp", None),
        P("dp", None),
        P("dp", "tensor"),
        P("dp", "tensor"),
        P("dp", "tensor"),
        P("tensor", "dp"),
        P("dp", "tensor"),
        P("dp", "tensor"),
        P("tensor", "dp"),
        P("dp"),
        P("dp"),
        P("dp", "tensor"),
        P(),
        P("dp", None),
    )
    out_specs = (
        P("dp", None),
        P("dp", None),
        P("dp", "tensor"),
        P("dp", "tensor"),
        P("dp", "tensor"),
        P("tensor", "dp"),
        P("dp", "tensor"),
        P("dp", "tensor"),
        P("tensor", "dp"),
        P("dp"),
        P("dp"),
        P("dp", "tensor"),
    )
    return jax.shard_map(
        functools.partial(per_device, sizes),
        mesh=mesh,
        in_specs=in_specs,
        out_specs=out_specs,
        check_vma=False,
    )
```

time: 993 us -> 359 us (0.36)
  blocking collectives: 281 us -> 21.6 us
  waiting for transfers between devices: 407 us -> 172 us
  other arithmetic: 193 us -> 17.8 us
  Pallas kernels: 0 us -> 65.1 us
  matrix products: 70.6 us -> 34.9 us
    reduce_scatter x7 -> x0, waiting for transfers between devices: 316 us -> none  [the longest x1 62.7 us: per_device(): lax.psum_scatter(grad_down.astype(jnp.bfloat16), 'dp', scatter_dimension=...]
    all_gather x8 -> x0, blocking collectives: 238 us -> none  [the longest x1 33.3 us: per_device(): lax.all_gather(w_down.astype(jnp.bfloat16), 'dp', axis=1, tiled=True)]
    reduce_sum x5 -> x1, other arithmetic: 117 us -> 1.75 us  [per_device(): jnp.sum(bg.reshape(8, 32, 4, heads, 32), axis=(1, 4))]
    pallas_call x0 -> x2, Pallas kernels: none -> 65.1 us  [the longest x1 47.7 us: per_device(): pl.pallas_call(functools.partial(first_kernel, sizes, heads), out_shape=s...]
    eq x3 -> x0, other arithmetic: 42.2 us -> none  [the longest x1 22.3 us: bias_lookup(): matches = buckets[None, None, :, :] == bucket_ids[:, None, None, None]]
    unnamed x10 -> x5, waiting for transfers between devices: 0.16 us -> 42 us
    dot_general x35 -> x18, matrix products: 70.6 us -> 34.9 us  [dot(): return lax.dot_general(former, latter, dims, preferred_element_type=F32)]
    psum x2, waiting for transfers between devices: 52.3 us -> 81.9 us  [the longest x1 48.8 us: per_device(): middle = inputs + lax.psum(dot(head_mix, out_t, NT), 'tensor')]
  transfers between devices with their start and end apart: 10 -> 4, of which waited for: 8 -> 4; matrix products, arithmetic and copies ran while one was open for 14% -> 8% of each run, Pallas kernels for 0% -> 0%
where the time goes in v1:
time: 359 us; the launch traced here: 358 us
  waiting for transfers between devices  172 us (48%)
  Pallas kernels  65.1 us (18%)
  matrix products  34.9 us (10%)
  local copies, waits for them, and re-layouts  30.3 us (8%)
  blocking collectives  21.6 us (6%)
  other arithmetic  17.8 us (5%)
  between operations  15.4 us (4%)
    psum x1, waiting for transfers between devices, per_device(): middle = inputs + lax.psum(dot(head_mix, out_t, NT), 'tensor')  48.8 us
    psum x1, waiting for transfers between devices, per_device(): grad_normed_ffn = lax.psum(partial_ffn, 'tensor')  48.3 us
    pallas_call x1, Pallas kernels, per_device(): pl.pallas_call(functools.partial(first_kernel, sizes, heads), out_shape=s...  47.7 us
    unnamed x5, waiting for transfers between devices  42 us
    dot_general x18, matrix products, dot(): return lax.dot_general(former, latter, dims, preferred_element_type=F32)  34.9 us
    psum x1, waiting for transfers between devices, per_device(): ffn_out = lax.psum(dot(hidden, down_t, NT).astype(BF), 'tensor').astype(F32)  33.1 us
    unnamed x1, blocking collectives  21.6 us
    unnamed x69, local copies, waits for them, and re-layouts  20 us
  transfers between devices with their start and end apart: 4, of which 4 were waited for; matrix products, arithmetic and copies ran while one was open for 8% of the time, Pallas kernels for 0%

profile of v1, /device:TPU:0, one launch (start us, length us, event | category | flops | bytes accessed | tf_op | source)
XLA Modules:
  0.0 357.9 jit_solution(11508523624942656750)
XLA Ops:
  11.8 47.7 %gather_attend.1 = (bf16[8,64,384]{2,1,0:T(8,128)(2,1)}, bf16[8,64,128]{2,1,0:T(8,128)(2,1)}, bf16[8,64,512]{2,1,0:T(8,128)(2,1)}, bf16[8,64,512]{2,1,0:T(8,128)...) custom-call(bf16[1024,512]{1,0:T(8,128)(2,1)} %x_hbm.1, ...), custom_call_target="tpu_custom_call" | custom-call | tf_op jit(solution)/shard_map/gather_attend/pallas_call | solution.py:406
  63.6 48.8 %all-reduce.9.cloned.1.call-done = f32[1024,512]{1,0:T(8,128)} async-done(((f32[1024,512]{1,0:T(8,128)}), f32[1024,512]{1,0:T(8,128)}) %all-reduce.9.cloned.1.call-update) | async-done | bytes 2097168 | tf_op jit(solution)/shard_map/psum | solution.py:456
  112.4 2.1 multiply_reduce_fusion.2
  117.6 2.9 fusion.13
  121.9 2.1 convolution_add_fusion
  124.3 3.1 convolution_convert_fusion
  127.4 48.3 %all-reduce.11.cloned.1.call-done = f32[1024,512]{1,0:T(8,128)} async-done(((f32[1024,512]{1,0:T(8,128)}), f32[1024,512]{1,0:T(8,128)}) %all-reduce.11.cloned.1.call-update) | async-done | bytes 2097168 | tf_op jit(solution)/shard_map/psum | solution.py:473
  175.6 2.9 multiply_reduce_fusion
  181.7 2.0 copy.75
  183.6 17.4 %attend_back.1 = (bf16[2,1024,64]{2,1,0:T(8,128)(2,1)}, bf16[2,1024,64]{2,1,0:T(8,128)(2,1)}, bf16[2,1024,64]{2,1,0:T(8,128)(2,1)}, f32[256,256]{1,0:T(8,128)}) custom-call(bf16[2,1024,64]{2,1,0:T(8,128)(2,1)} %get-tuple-element.34.q_v, bf16[2,1024,64]{2,1,0:T(8,128)(2,1)} %get-tuple-element.35.k_v, bf16[2,1024,64]{2,1,0:T(8,128)(2,1)} %get-tuple-element.36.v_v, ...), custom_call_target="tpu_custom_call" | custom-call | tf_op jit(solution)/shard_map/attend_back/pallas_call | solution.py:483
  202.9 1.9 copy.76
  204.9 2.8 fusion.25
  207.7 2.7 fusion.27
  210.4 1.9 copy.78
  212.3 2.4 fusion.21
  214.8 2.3 fusion.20
  218.0 3.2 add_convert_fusion
  221.5 2.7 fusion.18
  229.3 4.0 %copy.89 = bf16[512,2048]{1,0:T(8,128)(2,1)} copy(bf16[512,2048]{0,1:T(8,128)(2,1)} %fusion.17) | data formatting | bytes 4194304
  239.9 33.1 %all-reduce.13.cloned.1.call-done = (bf16[1024,512]{1,0:T(8,128)(2,1)}, bf16[1024,512]{1,0:T(8,128)(2,1)}) async-done(((bf16[1024,512]{1,0:T(8,128)(2,1)}, bf16[1024,512]{1,0:T(8,128)(2,1)}), (bf16[1024,512]{1,0:T(8,128)(2,1)}, bf16[1024,512]{1,0:T(8,128)(2,1)})) %all-reduce.13.cloned.1.call-update) | async-done | bytes 2097168 | tf_op jit(solution)/shard_map/psum | solution.py:461
  273.0 2.3 fusion.1
  275.3 21.6 %all-reduce.3 = (bf16[512]{0:T(512)(128)(2,1)S(1)}, bf16[512]{0:T(512)(128)(2,1)S(1)}, bf16[32,2]{0,1:T(2,128)(2,1)S(1)}) all-reduce(bf16[512]{0:T(512)(128)(2,1)S(1)} %get-tuple-element.94, bf16[512]{0:T(512)(128)(2,1)S(1)} %copy-done.24, bf16[32,2]{0,1:T(2,128)(2,1)S(1)} %convert_element_type.164), channel_id=3, replica_groups=mesh['dp'=8,'tensor'=4] {'dp'}, use_global_device_ids=true, to_apply=%region_10.0.clone | all-reduce | flops 1088 | bytes 4352
  298.2 2.7 add_convert_fusion.1
  302.9 41.9 %reduce-scatter.5.cloned.1.call-done = bf16[64,2048]{1,0:T(8,128)(2,1)} async-done(((bf16[512,2048]{1,0:T(8,128)(2,1)}), bf16[64,2048]{1,0:T(8,128)(2,1)}) %reduce-scatter.5.cloned.1.call-update) | async-done | bytes 262160
  (111 shorter events, 39.6 us)
Async XLA Ops:
  7.2 105.2 %all-reduce.9.cloned.1.call-start = ((), (), s32[]{:S(2)}) async-start(), calls=%async_computation.1 | async-start | bytes 4194304 | tf_op jit(solution)/shard_map/psum | solution.py:456
  59.5 1.5 copy-start.20
  61.1 1.9 copy-start.22
  61.1 51.4 %copy-start.2 = (bf16[1024,512]{1,0:T(8,128)(2,1)S(1)}, bf16[1024,512]{1,0:T(8,128)(2,1)}, u32[]{:S(2)}) copy-start(bf16[1024,512]{1,0:T(8,128)(2,1)} %x_hbm.1) | copy-start | bytes 3145732
  62.9 112.8 %all-reduce.11.cloned.1.call-start = ((), (), s32[]{:S(2)}) async-start(), calls=%async_computation.2 | async-start | bytes 4194304 | tf_op jit(solution)/shard_map/psum | solution.py:473
  114.8 2.2 copy-start.3
  114.8 1.5 copy-start.11
  124.0 149.0 %all-reduce.13.cloned.1.call-start = ((), (), s32[]{:S(2)}) async-start(), calls=%async_computation.4 | async-start | bytes 4194304 | tf_op jit(solution)/shard_map/psum | solution.py:461
  175.6 2.9 copy-start.6
  175.6 2.9 copy-start.14
  204.9 2.8 copy-start.10
  212.3 4.7 %copy-start.5 = (bf16[1024,512]{1,0:T(8,128)(2,1)S(1)}, bf16[1024,512]{1,0:T(8,128)(2,1)}, u32[]{:S(2)}) copy-start(bf16[1024,512]{1,0:T(8,128)(2,1)} %get-tuple-element.42) | copy-start | bytes 3145732
  212.3 4.7 %copy-start.9 = (bf16[1024,2,64]{0,2,1:T(8,128)(2,1)S(1)}, bf16[1024,2,64]{0,2,1:T(8,128)(2,1)}, u32[]{:S(2)}) copy-start(bf16[1024,2,64]{0,2,1:T(8,128)(2,1)} %copy.78) | copy-start | bytes 786436
  212.3 5.6 %copy-start.7 = (f32[1024,512]{1,0:T(8,128)S(1)}, f32[1024,512]{1,0:T(8,128)}, u32[]{:S(2)}) copy-start(f32[1024,512]{1,0:T(8,128)} %fusion.25) | copy-start | bytes 6291460
  221.2 123.6 %reduce-scatter.5.cloned.1.call-start = ((), (), s32[]{:S(2)}) async-start(), calls=%async_computation.3 | async-start | bytes 2359296
  221.5 2.7 copy-start.4
  221.5 2.7 copy-start.17
  224.2 1.6 copy-start.19
  225.8 1.6 copy-start.15
  225.8 2.0 copy-start.27
  233.3 2.7 copy-start.21
  236.0 39.3 %copy-start.24 = (bf16[512]{0:T(512)(128)(2,1)S(1)}, bf16[512]{0:T(512)(128)(2,1)}, u32[]{:S(2)}) copy-start(bf16[512]{0:T(512)(128)(2,1)} %get-tuple-element.92) | copy-start | bytes 3076
  298.2 2.8 copy-start.1
  298.2 2.8 copy-start.8
  (8 other events, 8.7 us)
Sparse Core Ops, SparseCore 0:
  63.0 49.3 all-reduce.8
  124.1 51.4 all-reduce.10
  221.3 51.6 all-reduce.12
  276.8 67.9 reduce-scatter.4

commit v2 on v1

v2 whole, which is shorter than its diff:
```python
import functools
import types

import jax
import jax.numpy as jnp
from jax import lax
from jax.experimental import pallas as pl
from jax.experimental.pallas import tpu as pltpu
from jax.sharding import PartitionSpec as P

MESH = pl.DeviceIdType.MESH
BF = jnp.bfloat16
F32 = jnp.float32
NN = (((1,), (0,)), ((), ()))
NT = (((1,), (1,)), ((), ()))
TN = (((0,), (0,)), ((), ()))
epsilon = 1e-06
masked_score = -1000000000.0
LANES = 128
BUCKETS = 32
LOW = 4
GROUP = 32
BLOCK = 256
SUB = 128
gelu_scale = 0.7978845608028654
gelu_cube = 0.044715


def dot(former, latter, dims, **more):
    return lax.dot_general(former, latter, dims, preferred_element_type=F32, **more)


def rows_of(index, size):
    return pl.ds(pl.multiple_of(index * size, size), size)


def lookup(table, ids):
    tiles = ids.shape[1] // LANES
    return jnp.concatenate(
        [
            jnp.take_along_axis(table, ids[:, c * LANES : (c + 1) * LANES], axis=1)
            for c in range(tiles)
        ],
        axis=1,
    )


def inverse_rms(values):
    return lax.rsqrt(jnp.mean(values * values, axis=1, keepdims=True) + epsilon)


def norm_back(grad_normed, values, gain):
    r = inverse_rms(values)
    u = grad_normed * gain
    return r * u - values * (r * r * r) * jnp.mean(u * values, axis=1, keepdims=True)


class Comm:
    def __init__(self, sizes, sems):
        self.Z, self.Y, self.X = sizes
        self.sems = sems
        self.used = 0
        self.d, self.t = lax.axis_index("dp"), lax.axis_index("tensor")
        self.z, self.y = self.d // self.Y, self.d % self.Y
        self.x, self.c = self.t // 2, self.t % 2
        self.pending = []

    def z_peer(self, k):
        return ((self.z + k) % self.Z) * self.Y + self.y, self.t

    def y_peer(self, j):
        return self.z * self.Y + (self.y + j) % self.Y, self.t

    def x_to(self, j, other=0):
        core = self.c if other == 0 else 1 - self.c
        return ((self.x + j) % self.X) * 2 + core

    def x_from(self, j, other=0):
        core = self.c if other == 0 else 1 - self.c
        return ((self.x - j) % self.X) * 2 + core

    def origin(self, kz, j=0):
        return ((self.z - kz) % self.Z) * self.Y + (self.y - j) % self.Y

    def pair(self):
        self.used += 2
        return self.sems.at[self.used - 2], self.sems.at[self.used - 1]

    def barrier(self):
        peers = [self.z_peer(k) for k in range(1, self.Z)]
        peers += [self.y_peer(j) for j in range(1, self.Y)]
        peers += [(self.d, self.x_to(j)) for j in range(1, self.X)]
        peers += [(self.d, self.x_to(j, 1)) for j in range(self.X)]
        semaphore = pltpu.get_barrier_semaphore()
        for peer in peers:
            pl.semaphore_signal(semaphore, inc=1, device_id=peer, device_id_type=MESH)
        pl.semaphore_wait(semaphore, len(peers))

    def copy(self, src, dst, peer, pair):
        return pltpu.make_async_remote_copy(
            src_ref=src,
            dst_ref=dst,
            send_sem=pair[0],
            recv_sem=pair[1],
            device_id=peer,
            device_id_type=MESH,
        )

    def send(self, src, dst, peer, pair):
        made = self.copy(src, dst, peer, pair)
        made.start()
        self.pending.append(made)

    def arrived(self, ref, peer, pair):
        self.copy(ref, ref, peer, pair).wait_recv()

    def drain(self):
        for made in self.pending:
            made.wait_send()
        self.pending = []


class Gather:
    def __init__(self, comm, full):
        self.comm, self.full = comm, full
        Z, Y = comm.Z, comm.Y
        self.zp = {k: comm.pair() for k in range(1, Z)}
        self.yp = {(k, j): comm.pair() for k in range(Z) for j in range(1, Y)}

    def send_y(self, k):
        m = self.comm
        block = self.full.at[m.origin(k)]
        for j in range(1, m.Y):
            m.send(block, block, m.y_peer(j), self.yp[k, j])

    def start(self):
        m = self.comm
        own = self.full.at[m.d]
        for k in range(m.Z - 1, 0, -1):
            m.send(own, own, m.z_peer(k), self.zp[k])
        self.send_y(0)

    def forward(self):
        m = self.comm
        for k in range(1, m.Z):
            m.arrived(self.full.at[m.origin(k)], m.z_peer(k), self.zp[k])
            self.send_y(k)

    def finish(self):
        m = self.comm
        for k in range(m.Z):
            for j in range(1, m.Y):
                m.arrived(self.full.at[m.origin(k, j)], m.y_peer(j), self.yp[k, j])


class Share:
    def __init__(self, comm, part):
        self.comm, self.part = comm, part
        self.xp = {j: comm.pair() for j in range(1, comm.X)}
        self.cp = {j: comm.pair() for j in range(comm.X)}

    def send_core(self, j):
        m = self.comm
        ref = self.part(m.x_from(j))
        m.send(ref, ref, (m.d, m.x_to(0, 1)), self.cp[j])

    def start(self):
        m = self.comm
        ref = self.part(m.t)
        for j in range(1, m.X):
            m.send(ref, ref, (m.d, m.x_to(j)), self.xp[j])
        self.send_core(0)

    def forward(self):
        m = self.comm
        for j in range(1, m.X):
            m.arrived(self.part(m.x_from(j)), (m.d, m.x_to(j)), self.xp[j])
            self.send_core(j)

    def finish(self):
        m = self.comm
        for j in range(m.X):
            m.arrived(self.part(m.x_from(j, 1)), (m.d, m.x_to(0, 1)), self.cp[j])


class Scatter:
    def __init__(self, comm, part, from_y, mine, from_z):
        self.comm, self.part, self.from_y, self.mine, self.from_z = comm, part, from_y, mine, from_z
        self.yp = {j: comm.pair() for j in range(1, comm.Y)}
        self.zp = {k: comm.pair() for k in range(1, comm.Z)}

    def start(self):
        m = self.comm
        for j in range(1, m.Y):
            src = self.part.at[:, (m.y + j) % m.Y]
            m.send(src, self.from_y.at[j - 1], m.y_peer(j), self.yp[j])

    def middle(self):
        m = self.comm
        for j in range(1, m.Y):
            m.arrived(self.from_y.at[j - 1], m.y_peer(j), self.yp[j])
        total = self.part[:, m.y].astype(F32)
        for j in range(1, m.Y):
            total = total + self.from_y[j - 1].astype(F32)
        self.mine[...] = total.astype(self.mine.dtype)
        for k in range(1, m.Z):
            m.send(self.mine.at[(m.z + k) % m.Z], self.from_z.at[k - 1], m.z_peer(k), self.zp[k])

    def finish(self):
        m = self.comm
        total = self.mine[m.z].astype(F32)
        for k in range(1, m.Z):
            m.arrived(self.from_z.at[k - 1], m.z_peer(k), self.zp[k])
            total = total + self.from_z[k - 1].astype(F32)
        return total


class Halves:
    def __init__(self, comm, block, away, kept, near, far):
        self.comm, self.block = comm, block
        self.away, self.kept, self.near, self.far = away, kept, near, far
        self.cp = comm.pair()
        self.xp = {j: comm.pair() for j in range(1, comm.X)}

    def start(self, values):
        m, b = self.comm, self.block
        half = BLOCK // 2
        self.away[b] = values[:half].astype(BF)
        self.kept[b] = values[half:]
        m.send(self.away.at[b], self.near.at[b], (m.d, m.x_to(0, 1)), self.cp)

    def middle(self):
        m, b = self.comm, self.block
        m.arrived(self.near.at[b], (m.d, m.x_to(0, 1)), self.cp)
        self.far[m.x, b] = (self.kept[b] + self.near[b].astype(F32)).astype(BF)
        for j in range(1, m.X):
            ref = self.far.at[m.x, b]
            m.send(ref, ref, (m.d, m.x_to(j)), self.xp[j])

    def finish(self):
        m, b = self.comm, self.block
        for j in range(1, m.X):
            m.arrived(self.far.at[(m.x - j) % m.X, b], (m.d, m.x_to(j)), self.xp[j])
        total = self.far[0, b].astype(F32)
        for j in range(1, m.X):
            total = total + self.far[j, b].astype(F32)
        return total


def layer_kernel(sizes, heads, names, *refs):
    r = types.SimpleNamespace(**dict(zip(names, refs)))
    T, D = r.x.shape
    dp, R, I = r.wq_all.shape[1:]
    F = r.wg.shape[2]
    NT_ = r.wq_all.shape[0]
    BR = BUCKETS // dp
    HD = I // heads
    NB = T // BLOCK
    half = BLOCK // 2
    sem_at = iter(range(1000))

    def local(src, dst):
        return pltpu.make_async_copy(src, dst, r.local_sems.at[next(sem_at)])

    early = [
        local(r.wq_in, r.s_attn.at[0]),
        local(r.wk_in, r.s_attn.at[1]),
        local(r.wv_in, r.s_attn.at[2]),
        local(r.ga_in, r.s_ga),
        local(r.gf_in, r.s_gf),
        local(r.bt_in, r.s_bt),
    ]
    load_o = local(r.wo_in, r.s_attn.at[3])
    load_f = [local(ref, r.s_ffn.at[n]) for n, ref in enumerate((r.wg_in, r.wu_in, r.wd_in))]
    load_x = local(r.x_in, r.x)
    load_b = local(r.bucket_in, r.buckets)
    load_p = local(r.pad_in, r.pad)
    load_g = local(r.g_in, r.g)
    for load in early + [load_o] + load_f + [load_x, load_b, load_p, load_g]:
        load.start()
    comm = Comm(sizes, r.sems)
    comm.barrier()
    d, t, c = comm.d, comm.t, comm.c
    attn_full = [ref.at[t] for ref in (r.wq_all, r.wk_all, r.wv_all)]
    g_qkv = [Gather(comm, f) for f in attn_full]
    g_misc = Gather(comm, r.misc)
    g_o = Gather(comm, r.wo_all.at[t])
    g_ffn = [Gather(comm, f) for f in (r.wg, r.wu, r.wd)]
    s_w = [
        Share(comm, lambda n, ref=ref: ref.at[n]) for ref in (r.wo_all, r.wq_all, r.wk_all, r.wv_all)
    ]
    s_mix = [Share(comm, lambda n, b=b: r.o_all.at[n, rows_of(b, BLOCK)]) for b in range(NB)]
    s_dq = [Share(comm, lambda n, b=b: r.dq_all.at[n, rows_of(b, BLOCK)]) for b in range(NB)]
    s_dk = Share(comm, lambda n: r.dk_all.at[n])
    s_dv = Share(comm, lambda n: r.dv_all.at[n])
    h_mid = [Halves(comm, b, r.m_away, r.m_kept, r.m_near, r.m_far) for b in range(NB)]
    h_out = [Halves(comm, b, r.f_away, r.f_kept, r.f_near, r.f_far) for b in range(NB)]
    p_dmb = [comm.pair() for _ in range(NB)]
    p_bo = [comm.pair() for _ in range(NB)]
    p_ig = [comm.pair() for _ in range(NB)]
    p_norm = {n: comm.pair() for n in range(1, NT_)}
    sc = {
        n: Scatter(comm, *[getattr(r, f"{kind}_{n}") for kind in ("part", "fy", "mine", "fz")])
        for n in "qkvogudm"
    }

    for load in early:
        load.wait()
    for n, ref in enumerate((r.wq_all, r.wk_all, r.wv_all)):
        ref[t, d] = r.s_attn[n].astype(BF)
    r.misc[d] = jnp.zeros(r.misc.shape[1:], F32)
    r.misc[d, 0:1, 0:R] = r.s_ga[...]
    r.misc[d, 1:2, 0:R] = r.s_gf[...]
    r.misc[d, 2 : 2 + heads, 0:BR] = r.s_bt[...]
    g_misc.start()
    for g in g_qkv:
        g.start()
    load_o.wait()
    r.wo_all[t, d] = r.s_attn[3].astype(BF)
    g_o.start()
    for n, (load, ref, g) in enumerate(zip(load_f, (r.wg, r.wu, r.wd), g_ffn)):
        load.wait()
        ref[d] = r.s_ffn[n].astype(BF)
        g.start()
    load_x.wait()
    load_b.wait()
    load_p.wait()
    load_g.wait()
    g_misc.forward()
    for g in g_qkv:
        g.forward()
    g_misc.finish()
    gains = jnp.concatenate([r.misc[n, :, 0:R] for n in range(dp)], axis=1).astype(BF).astype(F32)
    gain_attn, gain_ffn = gains[0:1], gains[1:2]
    lane = lax.broadcasted_iota(jnp.int32, (8, LANES), 1)
    table = jnp.zeros((8, LANES), F32)
    for n in range(dp):
        moved = r.misc[n] if n == 0 else pltpu.roll(r.misc[n], n * BR, 1)
        table = jnp.where(lane // BR == n, moved, table)
    table = table.astype(BF).astype(F32)[2 : 2 + heads]

    for g in g_qkv:
        g.finish()

    def project(b, carry):
        rows = rows_of(b, BLOCK)
        x = r.x[rows, :].astype(F32)
        n1 = (x * inverse_rms(x) * gain_attn).astype(BF)
        r.n1[rows, :] = n1
        for full, out in zip(attn_full, (r.q, r.k, r.v)):
            made = dot(n1, full[...].reshape(D, I), NN).astype(BF)
            for h in range(heads):
                out[h, rows, :] = made[:, h * HD : (h + 1) * HD]
        return carry

    lax.fori_loop(0, NB, project, 0)
    g_o.forward()
    g_ffn[0].forward()
    real = r.pad[...] > 0

    def attend(i, carry):
        rows = rows_of(i, SUB)
        ids = r.buckets[rows, :]
        mixed = []
        for h in range(heads):
            scores = dot(r.q[h, rows, :], r.k[h], NT)
            bias = lookup(jnp.broadcast_to(table[h : h + 1, :], (SUB, LANES)), ids)
            scores = jnp.where(real, scores + bias, masked_score)
            top = jnp.max(scores, axis=1, keepdims=True)
            e = jnp.exp(scores - top)
            p = (e * (1.0 / jnp.sum(e, axis=1, keepdims=True))).astype(BF)
            r.p[h, rows, :] = p
            mix = dot(p, r.v[h], NN)
            r.o[h, rows, :] = mix
            mixed.append(mix.astype(BF))
        r.o_all[t, rows, :] = jnp.concatenate(mixed, axis=1)
        return carry

    steps = BLOCK // SUB
    for b in range(NB):
        lax.fori_loop(b * steps, (b + 1) * steps, attend, 0)
        s_mix[b].start()
        if b > 0:
            s_mix[b - 1].forward()
        if b == 0:
            g_ffn[1].forward()
            g_o.finish()
            s_w[0].start()
        if b == 1:
            g_ffn[2].forward()
            s_w[0].forward()
        if b == 2:
            for s in s_w[1:]:
                s.start()
    s_w[0].finish()
    for n in range(NT_):
        r.wo_cat[:, n * I : (n + 1) * I] = r.wo_all[n].reshape(D, I)
    s_mix[NB - 1].forward()
    for g in g_ffn:
        g.finish()

    def feed(b):
        s_mix[b].finish()
        halves = [rows_of(2 * b + 1 - c, half), rows_of(2 * b + c, half)]

        def both(ref):
            return jnp.concatenate([ref[rows, :] for rows in halves], axis=0)

        def put(ref, values):
            ref[halves[0], :] = values[:half]
            ref[halves[1], :] = values[half:]

        mixed = jnp.concatenate(
            [
                jnp.concatenate([r.o_all[n, rows, :] for n in range(NT_)], axis=1)
                for rows in halves
            ],
            axis=0,
        )
        middle = both(r.x).astype(F32) + dot(mixed, r.wo_cat[...], NT)
        r.mid[b] = middle[half:]
        n2 = (middle * inverse_rms(middle) * gain_ffn).astype(BF)
        put(r.n2, n2)
        w_gate, w_up, w_down = [w[...].reshape(D, F) for w in (r.wg, r.wu, r.wd)]
        gate = dot(n2, w_gate, NN)
        up = dot(n2, w_up, NN)
        square = gate * gate
        th = jnp.tanh(gelu_scale * gate * (1.0 + gelu_cube * square))
        left = 0.5 * (1.0 + th)
        active = gate * left
        slope = left + 0.5 * gate * (1.0 - th * th) * (
            gelu_scale * (1.0 + 3.0 * gelu_cube * square)
        )
        hidden = (active * up).astype(BF)
        put(r.hidden, hidden)
        dhidden = dot(both(r.g), w_down, NN)
        dgate = (dhidden * up * slope).astype(BF)
        dup = (dhidden * active).astype(BF)
        put(r.dgate, dgate)
        put(r.dup, dup)
        h_mid[b].start(dot(dgate, w_gate, NT) + dot(dup, w_up, NT))
        h_out[b].start(dot(hidden, w_down, NT))

    def to_middle(b):
        rows = rows_of(2 * b + c, half)
        dn2 = h_mid[b].finish()
        dmiddle = r.g[rows, :].astype(F32) + norm_back(dn2, r.mid[b], gain_ffn)
        r.dmid[b] = dmiddle
        r.dmb[rows, :] = dmiddle.astype(BF)
        ref = r.dmb.at[rows]
        comm.send(ref, ref, (d, comm.x_to(0, 1)), p_dmb[b])

    def scatter_grad(name, values):
        part = getattr(r, "part_" + name)
        part[...] = values.astype(BF).reshape(part.shape)
        sc[name].start()

    for b in range(NB):
        feed(b)
        if b >= 1:
            h_mid[b - 1].middle()
        if b >= 2:
            to_middle(b - 2)
    scatter_grad("d", dot(r.g[...], r.hidden[...], TN))
    h_mid[NB - 1].middle()
    scatter_grad("g", dot(r.n2[...], r.dgate[...], TN))
    to_middle(NB - 2)
    scatter_grad("u", dot(r.n2[...], r.dup[...], TN))
    to_middle(NB - 1)
    for b in range(NB):
        h_out[b].middle()
    for s in s_w[1:]:
        s.forward()
    sc["d"].middle()
    for b in range(NB):
        comm.arrived(r.dmb.at[rows_of(2 * b + 1 - c, half)], (d, comm.x_to(0, 1)), p_dmb[b])

    w_out = r.wo_all[t].reshape(D, I)

    def mix_grad(b, carry):
        rows = rows_of(b, BLOCK)
        do = dot(r.dmb[rows, :], w_out, NN).astype(BF)
        for h in range(heads):
            r.do[h, rows, :] = do[:, h * HD : (h + 1) * HD]
        return carry

    lax.fori_loop(0, NB, mix_grad, 0)
    r.dv_all[t] = jnp.concatenate(
        [dot(r.p[h], r.do[h], TN).astype(BF) for h in range(heads)], axis=1
    )
    s_dv.start()
    scatter_grad("o", dot(r.dmb[...], r.o_all[t], TN))
    sc["g"].middle()
    scatter_grad("v", dot(r.n1[...], r.dv_all[t], TN))

    def back(i, carry):
        rows = rows_of(i, SUB)
        made = []
        for h in range(heads):
            do = r.do[h, rows, :]
            delta = jnp.sum(do.astype(F32) * r.o[h, rows, :], axis=1, keepdims=True)
            dprob = dot(do, r.v[h], NT)
            ds = (r.p[h, rows, :].astype(F32) * (dprob - delta)).astype(BF)
            r.ds[h, rows, :] = ds
            made.append(dot(ds, r.k[h], NN).astype(BF))
        r.dq_all[t, rows, :] = jnp.concatenate(made, axis=1)
        return carry

    def block_out(b):
        total = h_out[b].finish() + r.mid[b]
        r.s_bo[b] = total.astype(BF)
        ref = r.block_out.at[rows_of(2 * b + c, half)]
        comm.send(r.s_bo.at[b], ref, (d, comm.x_to(0, 1)), p_bo[b])
        return local(r.s_bo.at[b], ref)

    stores = []
    for b in range(NB):
        lax.fori_loop(b * steps, (b + 1) * steps, back, 0)
        s_dq[b].start()
        if b == 0:
            sc["u"].middle()
            s_dv.forward()
        if b == 1:
            sc["o"].middle()
        if b == 2:
            sc["v"].middle()
        if b > 0:
            s_dq[b - 1].forward()
        stores.append(block_out(b))
        stores[-1].start()
    r.dk_all[t] = jnp.concatenate(
        [dot(r.ds[h], r.q[h], TN).astype(BF) for h in range(heads)], axis=1
    )
    s_dk.start()
    scatter_grad("k", dot(r.n1[...], r.dk_all[t], TN))
    scatter_grad("q", dot(r.n1[...], r.dq_all[t], TN))
    s_dq[NB - 1].forward()

    r.bias_sum[...] = jnp.zeros(r.bias_sum.shape, F32)

    def bias_rows(i, carry):
        rows = rows_of(i, GROUP)
        ids = r.buckets[rows, :]
        high = (ids // LOW).astype(BF)
        low = (ids % LOW).astype(BF)
        one, zero = jnp.ones_like(high), jnp.zeros_like(high)
        former = jnp.concatenate(
            [jnp.where(high == BF(n), one, zero) for n in range(BUCKETS // LOW)], axis=0
        )
        latter = []
        for n in range(LOW):
            match = low == BF(n)
            latter += [jnp.where(match, r.ds[h, rows, :], zero) for h in range(heads)]
        r.bias_sum[...] += dot(former, jnp.concatenate(latter, axis=0), NT)
        return carry

    groups = T // GROUP
    lax.fori_loop(0, groups // 2, bias_rows, 0)
    s_dk.forward()
    lax.fori_loop(groups // 2, groups, bias_rows, 0)
    exact = dict(precision=lax.Precision.HIGHEST)
    tall, wide = r.bias_sum.shape
    row = lax.broadcasted_iota(jnp.int32, (tall, wide), 0)
    column = lax.broadcasted_iota(jnp.int32, (tall, wide), 1)
    sums = jnp.where(row % GROUP == column % GROUP, r.bias_sum[...], 0.0)
    sums = jnp.sum(sums.reshape(BUCKETS // LOW, GROUP, wide), axis=1)
    bucket = lax.broadcasted_iota(jnp.int32, (LANES, BUCKETS // LOW), 0)
    high = lax.broadcasted_iota(jnp.int32, (LANES, BUCKETS // LOW), 1)
    spread = jnp.where(bucket // LOW == high, 1.0, 0.0)
    spread = dot(spread, sums, NN, **exact)
    bucket = lax.broadcasted_iota(jnp.int32, (LANES, wide), 0)
    column = lax.broadcasted_iota(jnp.int32, (LANES, wide), 1)
    spread = jnp.where(bucket % LOW == column // (heads * GROUP), spread, 0.0)
    head = lax.broadcasted_iota(jnp.int32, (8, wide), 0)
    column = lax.broadcasted_iota(jnp.int32, (8, wide), 1)
    of_head = jnp.where(column // GROUP % heads == head, 1.0, 0.0)
    by_head = dot(of_head, spread, NT, **exact)
    for n in range(dp):
        moved = by_head if n == 0 else pltpu.roll(by_head, LANES - n * BR, 1)
        r.part_m[n // comm.Y, n % comm.Y] = moved
    sc["m"].start()
    sc["k"].middle()
    sc["q"].middle()

    for s in s_w[1:]:
        s.finish()
    s_dv.finish()
    for s in s_dq:
        s.finish()
    s_dk.finish()
    for b in range(NB):
        rows = rows_of(2 * b + c, half)
        dn1 = jnp.zeros((half, D), F32)
        for full, grads in zip((r.wq_all, r.wk_all, r.wv_all), (r.dq_all, r.dk_all, r.dv_all)):
            former = jnp.concatenate([grads[n, rows, :] for n in range(NT_)], axis=1)
            latter = jnp.concatenate([full[n].reshape(D, I) for n in range(NT_)], axis=1)
            dn1 = dn1 + dot(former, latter, NT)
        x = r.x[rows, :].astype(F32)
        r.s_ig[b] = r.dmid[b] + norm_back(dn1, x, gain_attn)
        ref = r.input_grad.at[rows]
        comm.send(r.s_ig.at[b], ref, (d, comm.x_to(0, 1)), p_ig[b])
        stores.append(local(r.s_ig.at[b], ref))
        stores[-1].start()
        if b == 0:
            sc["m"].middle()

    outs = {}
    for n, out in zip("dguovkq", (r.o_d, r.o_g, r.o_u, r.o_o, r.o_v, r.o_k, r.o_q)):
        value = sc[n].finish()
        ref = getattr(r, "s_" + n)
        ref[...] = value
        outs[n] = value
        stores.append(local(ref, out))
        stores[-1].start()

    def gain_grad(pairs, gain):
        total = jnp.zeros((8, R), F32)
        for weight, grad in pairs:
            product = weight.astype(F32) * grad
            total = total + dot(jnp.ones((8, product.shape[1]), F32), product, NT, **exact)
        return total[0:1] / gain.astype(BF).astype(F32)

    own = [ref[t, d] for ref in (r.wq_all, r.wk_all, r.wv_all)]
    r.norm[t] = jnp.zeros(r.norm.shape[1:], F32)
    r.norm[t, 0:1, 0:R] = gain_grad(list(zip(own, [outs[n] for n in "qkv"])), r.s_ga[...])
    r.norm[t, 1:2, 0:R] = gain_grad([(r.wg[d], outs["g"]), (r.wu[d], outs["u"])], r.s_gf[...])
    for n in range(1, NT_):
        ref = r.norm.at[t]
        comm.send(ref, ref, (d, (t + n) % NT_), p_norm[n])
    r.s_m[...] = sc["m"].finish()[0:heads, 0:BR]
    stores.append(local(r.s_m, r.o_m))
    stores[-1].start()
    for n in range(1, NT_):
        comm.arrived(r.norm.at[(t - n) % NT_], (d, (t + n) % NT_), p_norm[n])
    total = r.norm[0]
    for n in range(1, NT_):
        total = total + r.norm[n]
    r.s_na[...] = total[0:1, 0:R]
    r.s_nf[...] = total[1:2, 0:R]
    stores += [local(r.s_na, r.o_na), local(r.s_nf, r.o_nf)]
    for store in stores[-2:]:
        store.start()
    for b in range(NB):
        rows = rows_of(2 * b + 1 - c, half)
        comm.arrived(r.block_out.at[rows], (d, comm.x_to(0, 1)), p_bo[b])
        comm.arrived(r.input_grad.at[rows], (d, comm.x_to(0, 1)), p_ig[b])
    comm.drain()
    for store in stores:
        store.wait()


def per_device(
    sizes,
    tokens,
    cotangent,
    w_query,
    w_key,
    w_value,
    w_out,
    w_gate,
    w_up,
    w_down,
    norm_attn,
    norm_ffn,
    bias_table,
    buckets,
    padding,
):
    T, D = tokens.shape
    R, I = w_query.shape
    F = w_gate.shape[1]
    BR, heads = bias_table.shape
    HD = I // heads
    Z, Y, X = sizes
    dp, tensor = Z * Y, 2 * X
    NB, half = T // BLOCK, BLOCK // 2
    S, V = jax.ShapeDtypeStruct, pltpu.VMEM
    inputs = dict(
        x_in=tokens,
        g_in=cotangent,
        wq_in=w_query,
        wk_in=w_key,
        wv_in=w_value,
        wo_in=w_out.T,
        wg_in=w_gate,
        wu_in=w_up,
        wd_in=w_down.T,
        ga_in=norm_attn.reshape(1, R),
        gf_in=norm_ffn.reshape(1, R),
        bt_in=bias_table.T,
        bucket_in=buckets,
        pad_in=padding,
    )
    outputs = dict(
        block_out=S((T, D), BF),
        input_grad=S((T, D), F32),
        o_q=S((R, I), F32),
        o_k=S((R, I), F32),
        o_v=S((R, I), F32),
        o_o=S((R, I), F32),
        o_g=S((R, F), F32),
        o_u=S((R, F), F32),
        o_d=S((R, F), F32),
        o_na=S((1, R), F32),
        o_nf=S((1, R), F32),
        o_m=S((heads, BR), F32),
    )
    scratch = dict(
        s_attn=V((4, R, I), F32),
        s_ffn=V((3, R, F), F32),
        s_ga=V((1, R), F32),
        s_gf=V((1, R), F32),
        s_bt=V((heads, BR), F32),
        x=V((T, D), BF),
        g=V((T, D), BF),
        buckets=V((T, T), jnp.int32),
        pad=V((1, T), jnp.int32),
        misc=V((dp, 8, LANES), F32),
        wq_all=V((tensor, dp, R, I), BF),
        wk_all=V((tensor, dp, R, I), BF),
        wv_all=V((tensor, dp, R, I), BF),
        wo_all=V((tensor, dp, R, I), BF),
        wo_cat=V((D, tensor * I), BF),
        wg=V((dp, R, F), BF),
        wu=V((dp, R, F), BF),
        wd=V((dp, R, F), BF),
        n1=V((T, D), BF),
        q=V((heads, T, HD), BF),
        k=V((heads, T, HD), BF),
        v=V((heads, T, HD), BF),
        p=V((heads, T, T), BF),
        o=V((heads, T, HD), F32),
        o_all=V((tensor, T, I), BF),
        mid=V((NB, half, D), F32),
        n2=V((T, D), BF),
        hidden=V((T, F), BF),
        dgate=V((T, F), BF),
        dup=V((T, F), BF),
        m_away=V((NB, half, D), BF),
        m_kept=V((NB, half, D), F32),
        m_near=V((NB, half, D), BF),
        m_far=V((X, NB, half, D), BF),
        f_away=V((NB, half, D), BF),
        f_kept=V((NB, half, D), F32),
        f_near=V((NB, half, D), BF),
        f_far=V((X, NB, half, D), BF),
        dmid=V((NB, half, D), F32),
        dmb=V((T, D), BF),
        do=V((heads, T, HD), BF),
        ds=V((heads, T, T), BF),
        dq_all=V((tensor, T, I), BF),
        dk_all=V((tensor, T, I), BF),
        dv_all=V((tensor, T, I), BF),
        bias_sum=V((BUCKETS // LOW * GROUP, LOW * heads * GROUP), F32),
        s_bo=V((NB, half, D), BF),
        s_ig=V((NB, half, D), F32),
        norm=V((tensor, 8, LANES), F32),
        s_m=V((heads, BR), F32),
        s_na=V((1, R), F32),
        s_nf=V((1, R), F32),
    )
    widths = dict(q=I, k=I, v=I, o=I, g=F, u=F, d=F)
    for n, width in widths.items():
        scratch["part_" + n] = V((Z, Y, R, width), BF)
        scratch["fy_" + n] = V((Y - 1, Z, R, width), BF)
        scratch["mine_" + n] = V((Z, R, width), BF)
        scratch["fz_" + n] = V((Z - 1, R, width), BF)
        scratch["s_" + n] = V((R, width), F32)
    scratch["part_m"] = V((Z, Y, 8, LANES), F32)
    scratch["fy_m"] = V((Y - 1, Z, 8, LANES), F32)
    scratch["mine_m"] = V((Z, 8, LANES), F32)
    scratch["fz_m"] = V((Z - 1, 8, LANES), F32)
    gathers, shares = 8, 4 + 2 * NB + 2
    count = gathers * (Z - 1 + Z * (Y - 1)) + shares * (2 * X - 1) + 8 * (Y - 1 + Z - 1)
    count += 2 * NB * X + 3 * NB + tensor - 1
    scratch["local_sems"] = pltpu.SemaphoreType.DMA((14 + 2 * NB + 10,))
    scratch["sems"] = pltpu.SemaphoreType.DMA((2 * count,))
    names = [*inputs, *outputs, *scratch]
    made = pl.pallas_call(
        functools.partial(layer_kernel, sizes, heads, names),
        out_shape=list(outputs.values()),
        in_specs=[pl.BlockSpec(memory_space=pl.ANY)] * len(inputs),
        out_specs=[pl.BlockSpec(memory_space=pl.ANY)] * len(outputs),
        scratch_shapes=list(scratch.values()),
        compiler_params=pltpu.CompilerParams(
            collective_id=0, has_side_effects=True, vmem_limit_bytes=62 << 20
        ),
        name="layer",
    )(*inputs.values())
    out = dict(zip(outputs, made))
    return (
        out["block_out"],
        out["input_grad"],
        out["o_q"],
        out["o_k"],
        out["o_v"],
        out["o_o"].T,
        out["o_g"],
        out["o_u"],
        out["o_d"].T,
        out["o_na"].reshape(R),
        out["o_nf"].reshape(R),
        out["o_m"].T,
    )


def solution(mesh):
    shards, halves = mesh.shape["dp"], mesh.shape["tensor"]
    X = halves // 2
    Y = X if shards % X == 0 else 1
    sizes = (shards // Y, Y, X)
    in_specs = (
        P("dp", None),
        P("dp", None),
        P("dp", "tensor"),
        P("dp", "tensor"),
        P("dp", "tensor"),
        P("tensor", "dp"),
        P("dp", "tensor"),
        P("dp", "tensor"),
        P("tensor", "dp"),
        P("dp"),
        P("dp"),
        P("dp", "tensor"),
        P(),
        P("dp", None),
    )
    out_specs = (
        P("dp", None),
        P("dp", None),
        P("dp", "tensor"),
        P("dp", "tensor"),
        P("dp", "tensor"),
        P("tensor", "dp"),
        P("dp", "tensor"),
        P("dp", "tensor"),
        P("tensor", "dp"),
        P("dp"),
        P("dp"),
        P("dp", "tensor"),
    )
    return jax.shard_map(
        functools.partial(per_device, sizes),
        mesh=mesh,
        in_specs=in_specs,
        out_specs=out_specs,
        check_vma=False,
    )
```

time: 359 us -> 128 us (0.36)
  waiting for transfers between devices: 172 us -> 0 us
  Pallas kernels: 65.1 us -> 118 us
  matrix products: 34.9 us -> 0 us
  blocking collectives: 21.6 us -> 0 us
  local copies, waits for them, and re-layouts: 30.3 us -> 9.79 us
  other arithmetic: 17.8 us -> 0 us
  between operations: 15.4 us -> 0.74 us
    psum x3 -> x0, waiting for transfers between devices: 130 us -> none  [the longest x1 48.8 us: per_device(): middle = inputs + lax.psum(dot(head_mix, out_t, NT), 'tensor')]
    pallas_call x2 -> x1, Pallas kernels: 65.1 us -> 118 us  [per_device(): pl.pallas_call(functools.partial(layer_kernel, sizes, heads, names), out_...]
    unnamed x5 -> x0, waiting for transfers between devices: 42 us -> none
    dot_general x18 -> x0, matrix products: 34.9 us -> none  [dot(): return lax.dot_general(former, latter, dims, preferred_element_type=F32)]
    unnamed x1 -> x0, blocking collectives: 21.6 us -> none
    unnamed x69 -> x34, local copies, waits for them, and re-layouts: 20 us -> 9.79 us
    reduce_sum x4 -> x0, other arithmetic: 9.03 us -> none  [the longest x2 5.18 us: rms_scale(): values * lax.rsqrt(jnp.mean(values * values, axis=-1, keepdims=True) + ep...]
    convert_element_type x7 -> x0, other arithmetic: 6.23 us -> none  [the longest x1 2.74 us: per_device(): block_out = (middle + ffn_out).astype(BF)]
  transfers between devices with their start and end apart: 4 -> 0, of which waited for: 4 -> 0; matrix products, arithmetic and copies ran while one was open for 8% -> 0% of each run, Pallas kernels for 0% -> 0%
where the time goes in v2:
time: 128 us
  Pallas kernels  118 us (92%)
  local copies, waits for them, and re-layouts  9.79 us (8%)
    pallas_call x1, Pallas kernels, per_device(): pl.pallas_call(functools.partial(layer_kernel, sizes, heads, names), out_...  118 us
    unnamed x34, local copies, waits for them, and re-layouts  9.79 us

profile of v2, /device:TPU:0, one launch (start us, length us, event | category | flops | bytes accessed | tf_op | source)
XLA Modules:
  0.0 128.3 jit_solution(3107151015535020185)
XLA Ops:
  0.6 117.7 %layer.1 = (bf16[1024,512]{1,0:T(8,128)(2,1)}, f32[1024,512]{1,0:T(8,128)}, f32[64,128]{1,0:T(8,128)}, f32[64,128]{1,0:T(8,128)}, f32[64,128]{1,0:T(8,128)}, /*i...) custom-call(bf16[1024,512]{1,0:T(8,128)(2,1)} %refs_0_.1, ...), custom_call_target="tpu_custom_call" | custom-call | tf_op jit(solution)/shard_map/layer/pallas_call | solution.py:779
  118.4 0.0 copy-start
  118.4 2.4 %copy.38 = bf16[1024,512]{1,0:T(8,128)(2,1)} copy(bf16[1024,512]{1,0:T(8,128)(2,1)} %get-tuple-element.48) | data formatting | bytes 2097152
  120.8 0.0 copy-done
  120.8 0.0 copy-start.4
  120.8 0.0 copy-start.3
  120.9 0.0 copy-start.2
  120.9 0.0 copy-start.1
  120.9 0.0 copy-start.10
  120.9 0.0 copy-start.9
  120.9 0.0 copy-start.8
  120.9 1.3 %copy.39 = f32[1024,512]{1,0:T(8,128)} copy(f32[1024,512]{1,0:T(8,128)S(1)} %copy-done) | data formatting | bytes 4194304
  122.2 0.0 copy-done.7
  122.2 0.6 copy.40
  122.8 0.6 copy.41
  123.5 0.0 copy-done.5
  123.5 0.6 copy.42
  124.1 0.6 copy.43
  124.7 0.7 copy.44
  125.4 0.7 copy.45
  126.0 0.7 copy.46
  126.7 0.5 copy.47
  127.2 0.5 copy.48
  127.7 0.6 copy.49
  (11 shorter events, 0.0 us)
Async XLA Ops:
  118.4 2.4 %copy-start = (f32[1024,512]{1,0:T(8,128)S(1)}, f32[1024,512]{1,0:T(8,128)}, u32[]{:S(2)}) copy-start(f32[1024,512]{1,0:T(8,128)} %get-tuple-element.49) | copy-start | bytes 6291460
  120.8 1.4 %copy-start.7 = (f32[64,128]{1,0:T(8,128)S(1)}, f32[64,128]{1,0:T(8,128)}, u32[]{:S(2)}) copy-start(f32[64,128]{1,0:T(8,128)} %get-tuple-element.50) | copy-start | bytes 98308
  120.8 2.0 %copy-start.6 = (f32[64,128]{1,0:T(8,128)S(1)}, f32[64,128]{1,0:T(8,128)}, u32[]{:S(2)}) copy-start(f32[64,128]{1,0:T(8,128)} %get-tuple-element.51) | copy-start | bytes 98308
  120.8 2.6 %copy-start.5 = (f32[64,128]{1,0:T(8,128)S(1)}, f32[64,128]{1,0:T(8,128)}, u32[]{:S(2)}) copy-start(f32[64,128]{1,0:T(8,128)} %get-tuple-element.52) | copy-start | bytes 98308
  120.8 3.2 %copy-start.4 = (f32[64,128]{1,0:T(8,128)S(1)}, f32[64,128]{1,0:T(8,128)}, u32[]{:S(2)}) copy-start(f32[64,128]{1,0:T(8,128)} %get-tuple-element.29) | copy-start | bytes 98308
  120.8 3.9 %copy-start.3 = (f32[64,512]{1,0:T(8,128)S(1)}, f32[64,512]{1,0:T(8,128)}, u32[]{:S(2)}) copy-start(f32[64,512]{1,0:T(8,128)} %get-tuple-element.54) | copy-start | bytes 393220
  120.9 4.5 %copy-start.2 = (f32[64,512]{1,0:T(8,128)S(1)}, f32[64,512]{1,0:T(8,128)}, u32[]{:S(2)}) copy-start(f32[64,512]{1,0:T(8,128)} %get-tuple-element.55) | copy-start | bytes 393220
  120.9 5.2 %copy-start.1 = (f32[64,512]{1,0:T(8,128)S(1)}, f32[64,512]{1,0:T(8,128)}, u32[]{:S(2)}) copy-start(f32[64,512]{1,0:T(8,128)} %get-tuple-element.32) | copy-start | bytes 393220
  120.9 5.8 %copy-start.10 = (f32[1,64]{1,0:T(1,128)S(1)}, f32[1,64]{1,0:T(1,128)}, u32[]{:S(2)}) copy-start(f32[1,64]{1,0:T(1,128)} %get-tuple-element.33) | copy-start | bytes 772
  120.9 6.3 %copy-start.9 = (f32[1,64]{1,0:T(1,128)S(1)}, f32[1,64]{1,0:T(1,128)}, u32[]{:S(2)}) copy-start(f32[1,64]{1,0:T(1,128)} %get-tuple-element.34) | copy-start | bytes 772
  120.9 6.8 %copy-start.8 = (f32[2,4]{1,0:T(2,128)S(1)}, f32[2,4]{1,0:T(2,128)}, u32[]{:S(2)}) copy-start(f32[2,4]{1,0:T(2,128)} %get-tuple-element.35) | copy-start | bytes 100

commit v3 on v2

--- a/solution.py
+++ b/solution.py
@@ -22,6 +22,7 @@
 GROUP = 32
 BLOCK = 256
 SUB = 128
+GROUPS = 8
 gelu_scale = 0.7978845608028654
 gelu_cube = 0.044715
 
@@ -63,6 +64,7 @@
         self.d, self.t = lax.axis_index("dp"), lax.axis_index("tensor")
         self.z, self.y = self.d // self.Y, self.d % self.Y
         self.x, self.c = self.t // 2, self.t % 2
+        self.place = self.y * self.Z + self.z + (self.y % 2) * (self.Z - 1 - 2 * self.z)
         self.pending = []
 
     def z_peer(self, k):
@@ -81,6 +83,12 @@
 
     def origin(self, kz, j=0):
         return ((self.z - kz) % self.Z) * self.Y + (self.y - j) % self.Y
+
+    def ring(self, place):
+        count = self.Z * self.Y
+        place = (place + count) % count
+        y, z = place // self.Z, place % self.Z
+        return (z + (y % 2) * (self.Z - 1 - 2 * z)) * self.Y + y
 
     def pair(self):
         self.used += 2
@@ -91,6 +99,7 @@
         peers += [self.y_peer(j) for j in range(1, self.Y)]
         peers += [(self.d, self.x_to(j)) for j in range(1, self.X)]
         peers += [(self.d, self.x_to(j, 1)) for j in range(self.X)]
+        peers += [(self.ring(self.place + n), self.t) for n in (1, -1)]
         semaphore = pltpu.get_barrier_semaphore()
         for peer in peers:
             pl.semaphore_signal(semaphore, inc=1, device_id=peer, device_id_type=MESH)
@@ -153,6 +162,38 @@
                 m.arrived(self.full.at[m.origin(k, j)], m.y_peer(j), self.yp[k, j])
 
 
+class Ring:
+    def __init__(self, comm, full, turn):
+        self.comm, self.full = comm, full
+        count = comm.Z * comm.Y
+        most, least = count // 2, count - 1 - count // 2
+        self.reach = (most, least) if turn == 0 else (least, most)
+        self.pairs = [[comm.pair() for _ in range(n)] for n in self.reach]
+
+    def block(self, way, step):
+        m = self.comm
+        return self.full.at[m.ring(m.place - step if way == 0 else m.place + step)]
+
+    def pass_on(self, way, step):
+        m = self.comm
+        if step < self.reach[way]:
+            ref = self.block(way, step)
+            peer = m.ring(m.place + 1 if way == 0 else m.place - 1), m.t
+            m.send(ref, ref, peer, self.pairs[way][step])
+
+    def start(self):
+        for way in range(2):
+            self.pass_on(way, 0)
+
+    def step(self, step):
+        m = self.comm
+        for way in range(2):
+            if step <= self.reach[way]:
+                peer = m.ring(m.place + 1 if way == 0 else m.place - 1), m.t
+                m.arrived(self.block(way, step), peer, self.pairs[way][step - 1])
+                self.pass_on(way, step)
+
+
 class Share:
     def __init__(self, comm, part):
         self.comm, self.part = comm, part
@@ -250,9 +291,9 @@
 def layer_kernel(sizes, heads, names, *refs):
     r = types.SimpleNamespace(**dict(zip(names, refs)))
     T, D = r.x.shape
-    dp, R, I = r.wq_all.shape[1:]
-    F = r.wg.shape[2]
-    NT_ = r.wq_all.shape[0]
+    dp, R, I3 = r.wa.shape
+    I, F = r.wo_all.shape[3], r.wg.shape[2]
+    NT_ = r.wo_all.shape[0]
     BR = BUCKETS // dp
     HD = I // heads
     NB = T // BLOCK
@@ -272,49 +313,42 @@
     ]
     load_o = local(r.wo_in, r.s_attn.at[3])
     load_f = [local(ref, r.s_ffn.at[n]) for n, ref in enumerate((r.wg_in, r.wu_in, r.wd_in))]
-    load_x = local(r.x_in, r.x)
     load_b = local(r.bucket_in, r.buckets)
     load_p = local(r.pad_in, r.pad)
+    load_x = local(r.x_in, r.x)
     load_g = local(r.g_in, r.g)
-    for load in early + [load_o] + load_f + [load_x, load_b, load_p, load_g]:
+    for load in early + [load_o] + load_f + [load_b, load_p, load_x, load_g]:
         load.start()
     comm = Comm(sizes, r.sems)
     comm.barrier()
     d, t, c = comm.d, comm.t, comm.c
-    attn_full = [ref.at[t] for ref in (r.wq_all, r.wk_all, r.wv_all)]
-    g_qkv = [Gather(comm, f) for f in attn_full]
-    g_misc = Gather(comm, r.misc)
-    g_o = Gather(comm, r.wo_all.at[t])
-    g_ffn = [Gather(comm, f) for f in (r.wg, r.wu, r.wd)]
-    s_w = [
-        Share(comm, lambda n, ref=ref: ref.at[n]) for ref in (r.wo_all, r.wq_all, r.wk_all, r.wv_all)
-    ]
+    partner = (d, comm.x_to(0, 1))
+    g_misc, g_a, g_o = [Gather(comm, f) for f in (r.misc, r.wa, r.wo_all.at[t])]
+    g_ffn = [Ring(comm, f, n % 2) for n, f in enumerate((r.wg, r.wu, r.wd))]
+    s_wo = Share(comm, lambda n: r.wo_all.at[n])
     s_mix = [Share(comm, lambda n, b=b: r.o_all.at[n, rows_of(b, BLOCK)]) for b in range(NB)]
-    s_dq = [Share(comm, lambda n, b=b: r.dq_all.at[n, rows_of(b, BLOCK)]) for b in range(NB)]
-    s_dk = Share(comm, lambda n: r.dk_all.at[n])
-    s_dv = Share(comm, lambda n: r.dv_all.at[n])
     h_mid = [Halves(comm, b, r.m_away, r.m_kept, r.m_near, r.m_far) for b in range(NB)]
     h_out = [Halves(comm, b, r.f_away, r.f_kept, r.f_near, r.f_far) for b in range(NB)]
+    h_in = [Halves(comm, b, r.i_away, r.i_kept, r.i_near, r.i_far) for b in range(NB)]
     p_dmb = [comm.pair() for _ in range(NB)]
     p_bo = [comm.pair() for _ in range(NB)]
     p_ig = [comm.pair() for _ in range(NB)]
     p_norm = {n: comm.pair() for n in range(1, NT_)}
     sc = {
         n: Scatter(comm, *[getattr(r, f"{kind}_{n}") for kind in ("part", "fy", "mine", "fz")])
-        for n in "qkvogudm"
+        for n in "aogudm"
     }
 
     for load in early:
         load.wait()
-    for n, ref in enumerate((r.wq_all, r.wk_all, r.wv_all)):
-        ref[t, d] = r.s_attn[n].astype(BF)
+    for n in range(3):
+        r.wa[d, :, n * I : (n + 1) * I] = r.s_attn[n].astype(BF)
     r.misc[d] = jnp.zeros(r.misc.shape[1:], F32)
     r.misc[d, 0:1, 0:R] = r.s_ga[...]
     r.misc[d, 1:2, 0:R] = r.s_gf[...]
     r.misc[d, 2 : 2 + heads, 0:BR] = r.s_bt[...]
     g_misc.start()
-    for g in g_qkv:
-        g.start()
+    g_a.start()
     load_o.wait()
     r.wo_all[t, d] = r.s_attn[3].astype(BF)
     g_o.start()
@@ -322,13 +356,19 @@
         load.wait()
         ref[d] = r.s_ffn[n].astype(BF)
         g.start()
-    load_x.wait()
     load_b.wait()
     load_p.wait()
-    load_g.wait()
+
+    def split_bucket(i, carry):
+        rows = rows_of(i, SUB)
+        ids = r.buckets[rows, :]
+        r.high[rows, :] = (ids // LOW).astype(BF)
+        r.low[rows, :] = (ids % LOW).astype(BF)
+        return carry
+
+    lax.fori_loop(0, T // SUB, split_bucket, 0)
     g_misc.forward()
-    for g in g_qkv:
-        g.forward()
+    g_a.forward()
     g_misc.finish()
     gains = jnp.concatenate([r.misc[n, :, 0:R] for n in range(dp)], axis=1).astype(BF).astype(F32)
     gain_attn, gain_ffn = gains[0:1], gains[1:2]
@@ -338,66 +378,90 @@
         moved = r.misc[n] if n == 0 else pltpu.roll(r.misc[n], n * BR, 1)
         table = jnp.where(lane // BR == n, moved, table)
     table = table.astype(BF).astype(F32)[2 : 2 + heads]
-
-    for g in g_qkv:
-        g.finish()
+    real = r.pad[...] > 0
+
+    def fill_bias(i, carry):
+        rows = rows_of(i, SUB)
+        ids = r.buckets[rows, :]
+        for h in range(heads):
+            bias = lookup(jnp.broadcast_to(table[h : h + 1, :], (SUB, LANES)), ids)
+            r.ds[h, rows, :] = jnp.where(real, bias, masked_score).astype(BF)
+        return carry
+
+    lax.fori_loop(0, T // SUB // 2, fill_bias, 0)
+    g_o.forward()
+    g_ffn[0].step(1)
+    lax.fori_loop(T // SUB // 2, T // SUB, fill_bias, 0)
+    g_ffn[1].step(1)
+    load_x.wait()
+    load_g.wait()
+
+    g_a.finish()
 
     def project(b, carry):
         rows = rows_of(b, BLOCK)
         x = r.x[rows, :].astype(F32)
         n1 = (x * inverse_rms(x) * gain_attn).astype(BF)
         r.n1[rows, :] = n1
-        for full, out in zip(attn_full, (r.q, r.k, r.v)):
-            made = dot(n1, full[...].reshape(D, I), NN).astype(BF)
+        made = dot(n1, r.wa[...].reshape(D, I3), NN).astype(BF)
+        for n, out in enumerate((r.q, r.k, r.v)):
             for h in range(heads):
-                out[h, rows, :] = made[:, h * HD : (h + 1) * HD]
+                out[h, rows, :] = made[:, n * I + h * HD : n * I + (h + 1) * HD]
         return carry
 
     lax.fori_loop(0, NB, project, 0)
-    g_o.forward()
-    g_ffn[0].forward()
-    real = r.pad[...] > 0
-
-    def attend(i, carry):
-        rows = rows_of(i, SUB)
-        ids = r.buckets[rows, :]
-        mixed = []
+    g_ffn[2].step(1)
+    g_o.finish()
+    s_wo.start()
+
+    def mix(b):
+        rows = slice(b * BLOCK, (b + 1) * BLOCK)
+        return [dot(r.p[h, rows, :], r.v[h], NN) for h in range(heads)]
+
+    def put_mix(b, mixed):
+        rows = slice(b * BLOCK, (b + 1) * BLOCK)
         for h in range(heads):
-            scores = dot(r.q[h, rows, :], r.k[h], NT)
-            bias = lookup(jnp.broadcast_to(table[h : h + 1, :], (SUB, LANES)), ids)
-            scores = jnp.where(real, scores + bias, masked_score)
+            r.o[h, rows, :] = mixed[h]
+        r.o_all[t, rows, :] = jnp.concatenate([m.astype(BF) for m in mixed], axis=1)
+        s_mix[b].start()
+
+    for b in range(NB):
+        rows = slice(b * BLOCK, (b + 1) * BLOCK)
+        mixed = mix(b - 1) if b > 0 else None
+        weights = []
+        for h in range(heads):
+            scores = dot(r.q[h, rows, :], r.k[h], NT) + r.ds[h, rows, :].astype(F32)
             top = jnp.max(scores, axis=1, keepdims=True)
             e = jnp.exp(scores - top)
-            p = (e * (1.0 / jnp.sum(e, axis=1, keepdims=True))).astype(BF)
-            r.p[h, rows, :] = p
-            mix = dot(p, r.v[h], NN)
-            r.o[h, rows, :] = mix
-            mixed.append(mix.astype(BF))
-        r.o_all[t, rows, :] = jnp.concatenate(mixed, axis=1)
-        return carry
-
-    steps = BLOCK // SUB
-    for b in range(NB):
-        lax.fori_loop(b * steps, (b + 1) * steps, attend, 0)
-        s_mix[b].start()
+            weights.append((e * (1.0 / jnp.sum(e, axis=1, keepdims=True))).astype(BF))
+        for h in range(heads):
+            r.p[h, rows, :] = weights[h]
         if b > 0:
-            s_mix[b - 1].forward()
+            put_mix(b - 1, mixed)
         if b == 0:
-            g_ffn[1].forward()
-            g_o.finish()
-            s_w[0].start()
+            g_ffn[0].step(2)
+            g_ffn[1].step(2)
         if b == 1:
-            g_ffn[2].forward()
-            s_w[0].forward()
+            g_ffn[2].step(2)
+            s_wo.forward()
         if b == 2:
-            for s in s_w[1:]:
-                s.start()
-    s_w[0].finish()
+            g_ffn[0].step(3)
+            s_mix[0].forward()
+    put_mix(NB - 1, mix(NB - 1))
+    g_ffn[1].step(3)
+    s_mix[1].forward()
+    g_ffn[2].step(3)
+    s_mix[2].forward()
+    s_wo.finish()
     for n in range(NT_):
         r.wo_cat[:, n * I : (n + 1) * I] = r.wo_all[n].reshape(D, I)
-    s_mix[NB - 1].forward()
+    g_ffn[0].step(4)
+    s_mix[3].forward()
+    g_ffn[1].step(4)
+    g_ffn[2].step(4)
     for g in g_ffn:
-        g.finish()
+        for step in range(5, dp // 2 + 1):
+            g.step(step)
 
     def feed(b):
         s_mix[b].finish()
@@ -448,121 +512,99 @@
         r.dmid[b] = dmiddle
         r.dmb[rows, :] = dmiddle.astype(BF)
         ref = r.dmb.at[rows]
-        comm.send(ref, ref, (d, comm.x_to(0, 1)), p_dmb[b])
+        comm.send(ref, ref, partner, p_dmb[b])
 
     def scatter_grad(name, values):
         part = getattr(r, "part_" + name)
         part[...] = values.astype(BF).reshape(part.shape)
         sc[name].start()
 
+    w_out = r.wo_all[t].reshape(D, I)
+
+    def back(b):
+        comm.arrived(r.dmb.at[rows_of(2 * b + 1 - c, half)], partner, p_dmb[b])
+        rows = slice(b * BLOCK, (b + 1) * BLOCK)
+        do = dot(r.dmb[rows, :], w_out, NN).astype(BF)
+        made = []
+        for h in range(heads):
+            do_h = do[:, h * HD : (h + 1) * HD]
+            p = r.p[h, rows, :]
+            delta = jnp.sum(do_h.astype(F32) * r.o[h, rows, :], axis=1, keepdims=True)
+            ds = (p.astype(F32) * (dot(do_h, r.v[h], NT) - delta)).astype(BF)
+            r.ds[h, rows, :] = ds
+            made.append(dot(ds, r.k[h], NN).astype(BF))
+            more_k, more_v = dot(ds, r.q[h, rows, :], TN), dot(p, do_h, TN)
+            if b > 0:
+                more_k, more_v = r.dk[h] + more_k, r.dv[h] + more_v
+            r.dk[h], r.dv[h] = more_k, more_v
+        r.da[rows, 0:I] = jnp.concatenate(made, axis=1)
+        more = dot(r.dmb[rows, :], r.o_all[t, rows, :], TN)
+        r.go[...] = more if b == 0 else r.go[...] + more
+
     for b in range(NB):
         feed(b)
         if b >= 1:
             h_mid[b - 1].middle()
-        if b >= 2:
-            to_middle(b - 2)
     scatter_grad("d", dot(r.g[...], r.hidden[...], TN))
     h_mid[NB - 1].middle()
     scatter_grad("g", dot(r.n2[...], r.dgate[...], TN))
-    to_middle(NB - 2)
+    to_middle(0)
     scatter_grad("u", dot(r.n2[...], r.dup[...], TN))
-    to_middle(NB - 1)
+    for b in range(1, NB):
+        to_middle(b)
+        back(b - 1)
+        if b == 2:
+            sc["d"].middle()
+    h_out[0].middle()
+    back(NB - 1)
+    r.da[:, I : 2 * I] = jnp.concatenate([r.dk[h].astype(BF) for h in range(heads)], axis=1)
+    r.da[:, 2 * I : I3] = jnp.concatenate([r.dv[h].astype(BF) for h in range(heads)], axis=1)
+
     for b in range(NB):
+        halves = [rows_of(2 * b + 1 - c, half), rows_of(2 * b + c, half)]
+        former = jnp.concatenate([r.da[rows, :] for rows in halves], axis=0)
+        h_in[b].start(dot(former, r.wa[...].reshape(D, I3), NT))
+        if b >= 1:
+            h_in[b - 1].middle()
+    scatter_grad("a", dot(r.n1[...], r.da[...], TN))
+    h_in[NB - 1].middle()
+    scatter_grad("o", r.go[...])
+    sc["g"].middle()
+    for b in range(1, NB):
         h_out[b].middle()
-    for s in s_w[1:]:
-        s.forward()
-    sc["d"].middle()
-    for b in range(NB):
-        comm.arrived(r.dmb.at[rows_of(2 * b + 1 - c, half)], (d, comm.x_to(0, 1)), p_dmb[b])
-
-    w_out = r.wo_all[t].reshape(D, I)
-
-    def mix_grad(b, carry):
-        rows = rows_of(b, BLOCK)
-        do = dot(r.dmb[rows, :], w_out, NN).astype(BF)
-        for h in range(heads):
-            r.do[h, rows, :] = do[:, h * HD : (h + 1) * HD]
-        return carry
-
-    lax.fori_loop(0, NB, mix_grad, 0)
-    r.dv_all[t] = jnp.concatenate(
-        [dot(r.p[h], r.do[h], TN).astype(BF) for h in range(heads)], axis=1
-    )
-    s_dv.start()
-    scatter_grad("o", dot(r.dmb[...], r.o_all[t], TN))
-    sc["g"].middle()
-    scatter_grad("v", dot(r.n1[...], r.dv_all[t], TN))
-
-    def back(i, carry):
-        rows = rows_of(i, SUB)
-        made = []
-        for h in range(heads):
-            do = r.do[h, rows, :]
-            delta = jnp.sum(do.astype(F32) * r.o[h, rows, :], axis=1, keepdims=True)
-            dprob = dot(do, r.v[h], NT)
-            ds = (r.p[h, rows, :].astype(F32) * (dprob - delta)).astype(BF)
-            r.ds[h, rows, :] = ds
-            made.append(dot(ds, r.k[h], NN).astype(BF))
-        r.dq_all[t, rows, :] = jnp.concatenate(made, axis=1)
-        return carry
-
-    def block_out(b):
-        total = h_out[b].finish() + r.mid[b]
-        r.s_bo[b] = total.astype(BF)
-        ref = r.block_out.at[rows_of(2 * b + c, half)]
-        comm.send(r.s_bo.at[b], ref, (d, comm.x_to(0, 1)), p_bo[b])
-        return local(r.s_bo.at[b], ref)
-
-    stores = []
-    for b in range(NB):
-        lax.fori_loop(b * steps, (b + 1) * steps, back, 0)
-        s_dq[b].start()
-        if b == 0:
-            sc["u"].middle()
-            s_dv.forward()
-        if b == 1:
-            sc["o"].middle()
-        if b == 2:
-            sc["v"].middle()
-        if b > 0:
-            s_dq[b - 1].forward()
-        stores.append(block_out(b))
-        stores[-1].start()
-    r.dk_all[t] = jnp.concatenate(
-        [dot(r.ds[h], r.q[h], TN).astype(BF) for h in range(heads)], axis=1
-    )
-    s_dk.start()
-    scatter_grad("k", dot(r.n1[...], r.dk_all[t], TN))
-    scatter_grad("q", dot(r.n1[...], r.dq_all[t], TN))
-    s_dq[NB - 1].forward()
-
-    r.bias_sum[...] = jnp.zeros(r.bias_sum.shape, F32)
 
     def bias_rows(i, carry):
-        rows = rows_of(i, GROUP)
-        ids = r.buckets[rows, :]
-        high = (ids // LOW).astype(BF)
-        low = (ids % LOW).astype(BF)
-        one, zero = jnp.ones_like(high), jnp.zeros_like(high)
-        former = jnp.concatenate(
-            [jnp.where(high == BF(n), one, zero) for n in range(BUCKETS // LOW)], axis=0
+        former, latter = [], []
+        for g in range(GROUPS):
+            rows = rows_of(i * GROUPS + g, GROUP)
+            high, low = r.high[rows, :], r.low[rows, :]
+            one, zero = jnp.ones_like(high), jnp.zeros_like(high)
+            former.append(
+                jnp.concatenate(
+                    [jnp.where(high == BF(n), one, zero) for n in range(BUCKETS // LOW)], axis=0
+                )
+            )
+            part = []
+            for n in range(LOW):
+                match = low == BF(n)
+                part += [jnp.where(match, r.ds[h, rows, :], zero) for h in range(heads)]
+            latter.append(jnp.concatenate(part, axis=0))
+        return carry + dot(
+            jnp.concatenate(former, axis=1), jnp.concatenate(latter, axis=1), NT
         )
-        latter = []
-        for n in range(LOW):
-            match = low == BF(n)
-            latter += [jnp.where(match, r.ds[h, rows, :], zero) for h in range(heads)]
-        r.bias_sum[...] += dot(former, jnp.concatenate(latter, axis=0), NT)
-        return carry
-
-    groups = T // GROUP
-    lax.fori_loop(0, groups // 2, bias_rows, 0)
-    s_dk.forward()
-    lax.fori_loop(groups // 2, groups, bias_rows, 0)
+
+    count = T // (GROUP * GROUPS)
+    sums = lax.fori_loop(0, count // 2, bias_rows, jnp.zeros(r.bias_sum.shape, F32))
+    r.bias_sum[...] = sums
+    sc["a"].middle()
+    sc["u"].middle()
+    sums = r.bias_sum[...]
+    sums = lax.fori_loop(count // 2, count, bias_rows, sums)
     exact = dict(precision=lax.Precision.HIGHEST)
     tall, wide = r.bias_sum.shape
     row = lax.broadcasted_iota(jnp.int32, (tall, wide), 0)
     column = lax.broadcasted_iota(jnp.int32, (tall, wide), 1)
-    sums = jnp.where(row % GROUP == column % GROUP, r.bias_sum[...], 0.0)
+    sums = jnp.where(row % GROUP == column % GROUP, sums, 0.0)
     sums = jnp.sum(sums.reshape(BUCKETS // LOW, GROUP, wide), axis=1)
     bucket = lax.broadcasted_iota(jnp.int32, (LANES, BUCKETS // LOW), 0)
     high = lax.broadcasted_iota(jnp.int32, (LANES, BUCKETS // LOW), 1)
@@ -579,39 +621,34 @@
         moved = by_head if n == 0 else pltpu.roll(by_head, LANES - n * BR, 1)
         r.part_m[n // comm.Y, n % comm.Y] = moved
     sc["m"].start()
-    sc["k"].middle()
-    sc["q"].middle()
-
-    for s in s_w[1:]:
-        s.finish()
-    s_dv.finish()
-    for s in s_dq:
-        s.finish()
-    s_dk.finish()
+    sc["o"].middle()
+
+    stores = []
     for b in range(NB):
         rows = rows_of(2 * b + c, half)
-        dn1 = jnp.zeros((half, D), F32)
-        for full, grads in zip((r.wq_all, r.wk_all, r.wv_all), (r.dq_all, r.dk_all, r.dv_all)):
-            former = jnp.concatenate([grads[n, rows, :] for n in range(NT_)], axis=1)
-            latter = jnp.concatenate([full[n].reshape(D, I) for n in range(NT_)], axis=1)
-            dn1 = dn1 + dot(former, latter, NT)
         x = r.x[rows, :].astype(F32)
-        r.s_ig[b] = r.dmid[b] + norm_back(dn1, x, gain_attn)
+        r.s_ig[b] = r.dmid[b] + norm_back(h_in[b].finish(), x, gain_attn)
         ref = r.input_grad.at[rows]
-        comm.send(r.s_ig.at[b], ref, (d, comm.x_to(0, 1)), p_ig[b])
+        comm.send(r.s_ig.at[b], ref, partner, p_ig[b])
         stores.append(local(r.s_ig.at[b], ref))
         stores[-1].start()
         if b == 0:
             sc["m"].middle()
 
     outs = {}
-    for n, out in zip("dguovkq", (r.o_d, r.o_g, r.o_u, r.o_o, r.o_v, r.o_k, r.o_q)):
-        value = sc[n].finish()
-        ref = getattr(r, "s_" + n)
+
+    def keep(name, value, out):
+        ref = getattr(r, "s_" + name)
         ref[...] = value
-        outs[n] = value
         stores.append(local(ref, out))
         stores[-1].start()
+
+    for n, out in zip("dgu", (r.o_d, r.o_g, r.o_u)):
+        outs[n] = sc[n].finish()
+        keep(n, outs[n], out)
+    outs["a"] = sc["a"].finish()
+    for n, name, out in zip(range(3), "qkv", (r.o_q, r.o_k, r.o_v)):
+        keep(name, outs["a"][:, n * I : (n + 1) * I], out)
 
     def gain_grad(pairs, gain):
         total = jnp.zeros((8, R), F32)
@@ -620,31 +657,53 @@
             total = total + dot(jnp.ones((8, product.shape[1]), F32), product, NT, **exact)
         return total[0:1] / gain.astype(BF).astype(F32)
 
-    own = [ref[t, d] for ref in (r.wq_all, r.wk_all, r.wv_all)]
     r.norm[t] = jnp.zeros(r.norm.shape[1:], F32)
-    r.norm[t, 0:1, 0:R] = gain_grad(list(zip(own, [outs[n] for n in "qkv"])), r.s_ga[...])
+    r.norm[t, 0:1, 0:R] = gain_grad([(r.wa[d], outs["a"])], r.s_ga[...])
     r.norm[t, 1:2, 0:R] = gain_grad([(r.wg[d], outs["g"]), (r.wu[d], outs["u"])], r.s_gf[...])
     for n in range(1, NT_):
         ref = r.norm.at[t]
         comm.send(ref, ref, (d, (t + n) % NT_), p_norm[n])
-    r.s_m[...] = sc["m"].finish()[0:heads, 0:BR]
-    stores.append(local(r.s_m, r.o_m))
-    stores[-1].start()
+    keep("o", sc["o"].finish(), r.o_o)
+    keep("m", sc["m"].finish()[0:heads, 0:BR], r.o_m)
+    for b in range(NB):
+        rows = rows_of(2 * b + c, half)
+        total = h_out[b].finish() + r.mid[b]
+        r.s_bo[b] = total.astype(BF)
+        ref = r.block_out.at[rows]
+        comm.send(r.s_bo.at[b], ref, partner, p_bo[b])
+        stores.append(local(r.s_bo.at[b], ref))
+        stores[-1].start()
     for n in range(1, NT_):
         comm.arrived(r.norm.at[(t - n) % NT_], (d, (t + n) % NT_), p_norm[n])
     total = r.norm[0]
     for n in range(1, NT_):
         total = total + r.norm[n]
-    r.s_na[...] = total[0:1, 0:R]
-    r.s_nf[...] = total[1:2, 0:R]
-    stores += [local(r.s_na, r.o_na), local(r.s_nf, r.o_nf)]
-    for store in stores[-2:]:
-        store.start()
+    keep("na", total[0:1, 0:R], r.o_na)
+    keep("nf", total[1:2, 0:R], r.o_nf)
     for b in range(NB):
         rows = rows_of(2 * b + 1 - c, half)
-        comm.arrived(r.block_out.at[rows], (d, comm.x_to(0, 1)), p_bo[b])
-        comm.arrived(r.input_grad.at[rows], (d, comm.x_to(0, 1)), p_ig[b])
+        comm.arrived(r.block_out.at[rows], partner, p_bo[b])
+        comm.arrived(r.input_grad.at[rows], partner, p_ig[b])
     comm.drain()
+    for store in stores:
+        store.wait()
+
+
+def hand_over(*refs):
+    sems = refs[-1]
+    count = (len(refs) - 1) // 3
+    before, after, held = refs[:count], refs[count : 2 * count], refs[2 * count : 3 * count]
+    loads = [
+        pltpu.make_async_copy(a, b, sems.at[2 * n]) for n, (a, b) in enumerate(zip(before, held))
+    ]
+    stores = [
+        pltpu.make_async_copy(a, b, sems.at[2 * n + 1]) for n, (a, b) in enumerate(zip(held, after))
+    ]
+    for load in loads:
+        load.start()
+    for load, store in zip(loads, stores):
+        load.wait()
+        store.start()
     for store in stores:
         store.wait()
 
@@ -716,9 +775,9 @@
         buckets=V((T, T), jnp.int32),
         pad=V((1, T), jnp.int32),
         misc=V((dp, 8, LANES), F32),
-        wq_all=V((tensor, dp, R, I), BF),
-        wk_all=V((tensor, dp, R, I), BF),
-        wv_all=V((tensor, dp, R, I), BF),
+        wa=V((dp, R, 3 * I), BF),
+        high=V((T, T), BF),
+        low=V((T, T), BF),
         wo_all=V((tensor, dp, R, I), BF),
         wo_cat=V((D, tensor * I), BF),
         wg=V((dp, R, F), BF),
@@ -746,11 +805,15 @@
         f_far=V((X, NB, half, D), BF),
         dmid=V((NB, half, D), F32),
         dmb=V((T, D), BF),
-        do=V((heads, T, HD), BF),
+        i_away=V((NB, half, D), BF),
+        i_kept=V((NB, half, D), F32),
+        i_near=V((NB, half, D), BF),
+        i_far=V((X, NB, half, D), BF),
+        dk=V((heads, T, HD), F32),
+        dv=V((heads, T, HD), F32),
+        da=V((T, 3 * I), BF),
+        go=V((D, I), F32),
         ds=V((heads, T, T), BF),
-        dq_all=V((tensor, T, I), BF),
-        dk_all=V((tensor, T, I), BF),
-        dv_all=V((tensor, T, I), BF),
         bias_sum=V((BUCKETS // LOW * GROUP, LOW * heads * GROUP), F32),
         s_bo=V((NB, half, D), BF),
         s_ig=V((NB, half, D), F32),
@@ -759,20 +822,20 @@
         s_na=V((1, R), F32),
         s_nf=V((1, R), F32),
     )
-    widths = dict(q=I, k=I, v=I, o=I, g=F, u=F, d=F)
+    widths = dict(a=3 * I, o=I, g=F, u=F, d=F)
     for n, width in widths.items():
         scratch["part_" + n] = V((Z, Y, R, width), BF)
         scratch["fy_" + n] = V((Y - 1, Z, R, width), BF)
         scratch["mine_" + n] = V((Z, R, width), BF)
         scratch["fz_" + n] = V((Z - 1, R, width), BF)
+    for n, width in dict(q=I, k=I, v=I, o=I, g=F, u=F, d=F).items():
         scratch["s_" + n] = V((R, width), F32)
     scratch["part_m"] = V((Z, Y, 8, LANES), F32)
     scratch["fy_m"] = V((Y - 1, Z, 8, LANES), F32)
     scratch["mine_m"] = V((Z, 8, LANES), F32)
     scratch["fz_m"] = V((Z - 1, 8, LANES), F32)
-    gathers, shares = 8, 4 + 2 * NB + 2
-    count = gathers * (Z - 1 + Z * (Y - 1)) + shares * (2 * X - 1) + 8 * (Y - 1 + Z - 1)
-    count += 2 * NB * X + 3 * NB + tensor - 1
+    count = 3 * (Z - 1 + Z * (Y - 1)) + 3 * (dp - 1) + (1 + NB) * (2 * X - 1)
+    count += 3 * NB * X + 3 * NB + tensor - 1 + 6 * (Y + Z - 2)
     scratch["local_sems"] = pltpu.SemaphoreType.DMA((14 + 2 * NB + 10,))
     scratch["sems"] = pltpu.SemaphoreType.DMA((2 * count,))
     names = [*inputs, *outputs, *scratch]
@@ -787,6 +850,15 @@
         ),
         name="layer",
     )(*inputs.values())
+    made = pl.pallas_call(
+        hand_over,
+        out_shape=list(outputs.values()),
+        in_specs=[pl.BlockSpec(memory_space=pl.ANY)] * len(outputs),
+        out_specs=[pl.BlockSpec(memory_space=pl.ANY)] * len(outputs),
+        scratch_shapes=[V(o.shape, o.dtype) for o in outputs.values()]
+        + [pltpu.SemaphoreType.DMA((2 * len(outputs),))],
+        name="hand_over",
+    )(*made)
     out = dict(zip(outputs, made))
     return (
         out["block_out"],

time: 128 us -> 83.9 us (0.66)
  Pallas kernels: 118 us -> 82.9 us
  local copies, waits for them, and re-layouts: 9.79 us -> 0 us
    pallas_call x1, Pallas kernels: 118 us -> 79.3 us  [per_device(): pl.pallas_call(functools.partial(layer_kernel, sizes, heads, names), out_...]
    unnamed x34 -> x0, local copies, waits for them, and re-layouts: 9.79 us -> none
    pallas_call x0 -> x1, Pallas kernels: none -> 3.62 us  [per_device(): pl.pallas_call(hand_over, out_shape=list(outputs.values()), in_specs=[pl....]
where the time goes in v3:
time: 83.9 us; the launch traced here: 83.7 us
  Pallas kernels  82.9 us (99%)
  between operations  0.84 us (1%)
    pallas_call x1, Pallas kernels, per_device(): pl.pallas_call(functools.partial(layer_kernel, sizes, heads, names), out_...  79.3 us
    pallas_call x1, Pallas kernels, per_device(): pl.pallas_call(hand_over, out_shape=list(outputs.values()), in_specs=[pl....  3.62 us

profile of v3, /device:TPU:0, one launch (start us, length us, event | category | flops | bytes accessed | tf_op | source)
XLA Modules:
  0.0 83.7 jit_solution(18255641572621015036)
XLA Ops:
  0.6 79.3 %layer.1 = (bf16[1024,512]{1,0:T(8,128)(2,1)}, f32[1024,512]{1,0:T(8,128)}, f32[64,128]{1,0:T(8,128)}, f32[64,128]{1,0:T(8,128)}, f32[64,128]{1,0:T(8,128)}, /*i...) custom-call(bf16[1024,512]{1,0:T(8,128)(2,1)} %refs_0_.1, ...), custom_call_target="tpu_custom_call" | custom-call | tf_op jit(solution)/shard_map/layer/pallas_call | solution.py:842
  79.9 3.6 %hand_over.1 = (bf16[1024,512]{1,0:T(8,128)(2,1)}, f32[1024,512]{1,0:T(8,128)}, f32[64,128]{1,0:T(8,128)}, f32[64,128]{1,0:T(8,128)}, f32[64,128]{1,0:T(8,128)},...) custom-call(bf16[1024,512]{1,0:T(8,128)(2,1)} %get-tuple-element.36., ...), custom_call_target="tpu_custom_call" | custom-call | tf_op jit(solution)/shard_map/hand_over/pallas_call | solution.py:853

commit v4 on v3

--- a/solution.py
+++ b/solution.py
@@ -103,7 +103,7 @@
         semaphore = pltpu.get_barrier_semaphore()
         for peer in peers:
             pl.semaphore_signal(semaphore, inc=1, device_id=peer, device_id_type=MESH)
-        pl.semaphore_wait(semaphore, len(peers))
+        return lambda: pl.semaphore_wait(semaphore, len(peers))
 
     def copy(self, src, dst, peer, pair):
         return pltpu.make_async_remote_copy(
@@ -320,7 +320,7 @@
     for load in early + [load_o] + load_f + [load_b, load_p, load_x, load_g]:
         load.start()
     comm = Comm(sizes, r.sems)
-    comm.barrier()
+    all_here = comm.barrier()
     d, t, c = comm.d, comm.t, comm.c
     partner = (d, comm.x_to(0, 1))
     g_misc, g_a, g_o = [Gather(comm, f) for f in (r.misc, r.wa, r.wo_all.at[t])]
@@ -347,10 +347,11 @@
     r.misc[d, 0:1, 0:R] = r.s_ga[...]
     r.misc[d, 1:2, 0:R] = r.s_gf[...]
     r.misc[d, 2 : 2 + heads, 0:BR] = r.s_bt[...]
+    load_o.wait()
+    r.wo_all[t, d] = r.s_attn[3].astype(BF)
+    all_here()
     g_misc.start()
     g_a.start()
-    load_o.wait()
-    r.wo_all[t, d] = r.s_attn[3].astype(BF)
     g_o.start()
     for n, (load, ref, g) in enumerate(zip(load_f, (r.wg, r.wu, r.wd), g_ffn)):
         load.wait()
@@ -458,13 +459,11 @@
     g_ffn[0].step(4)
     s_mix[3].forward()
     g_ffn[1].step(4)
-    g_ffn[2].step(4)
-    for g in g_ffn:
-        for step in range(5, dp // 2 + 1):
-            g.step(step)
-
-    def feed(b):
-        s_mix[b].finish()
+    for step in range(5, dp // 2 + 1):
+        for g in g_ffn:
+            g.step(step - 1 if g is g_ffn[2] else step)
+
+    def halves_of(b):
         halves = [rows_of(2 * b + 1 - c, half), rows_of(2 * b + c, half)]
 
         def both(ref):
@@ -474,6 +473,11 @@
             ref[halves[0], :] = values[:half]
             ref[halves[1], :] = values[half:]
 
+        return halves, both, put
+
+    def feed(b):
+        s_mix[b].finish()
+        halves, both, put = halves_of(b)
         mixed = jnp.concatenate(
             [
                 jnp.concatenate([r.o_all[n, rows, :] for n in range(NT_)], axis=1)
@@ -485,7 +489,7 @@
         r.mid[b] = middle[half:]
         n2 = (middle * inverse_rms(middle) * gain_ffn).astype(BF)
         put(r.n2, n2)
-        w_gate, w_up, w_down = [w[...].reshape(D, F) for w in (r.wg, r.wu, r.wd)]
+        w_gate, w_up = [w[...].reshape(D, F) for w in (r.wg, r.wu)]
         gate = dot(n2, w_gate, NN)
         up = dot(n2, w_up, NN)
         square = gate * gate
@@ -497,6 +501,11 @@
         )
         hidden = (active * up).astype(BF)
         put(r.hidden, hidden)
+        return hidden, up, active, slope
+
+    def feed_back(b, hidden, up, active, slope):
+        halves, both, put = halves_of(b)
+        w_gate, w_up, w_down = [w[...].reshape(D, F) for w in (r.wg, r.wu, r.wd)]
         dhidden = dot(both(r.g), w_down, NN)
         dgate = (dhidden * up * slope).astype(BF)
         dup = (dhidden * active).astype(BF)
@@ -542,7 +551,10 @@
         r.go[...] = more if b == 0 else r.go[...] + more
 
     for b in range(NB):
-        feed(b)
+        made = feed(b)
+        if b == 0:
+            g_ffn[2].step(dp // 2)
+        feed_back(b, *made)
         if b >= 1:
             h_mid[b - 1].middle()
     scatter_grad("d", dot(r.g[...], r.hidden[...], TN))
@@ -600,7 +612,6 @@
     sc["u"].middle()
     sums = r.bias_sum[...]
     sums = lax.fori_loop(count // 2, count, bias_rows, sums)
-    exact = dict(precision=lax.Precision.HIGHEST)
     tall, wide = r.bias_sum.shape
     row = lax.broadcasted_iota(jnp.int32, (tall, wide), 0)
     column = lax.broadcasted_iota(jnp.int32, (tall, wide), 1)
@@ -609,14 +620,14 @@
     bucket = lax.broadcasted_iota(jnp.int32, (LANES, BUCKETS // LOW), 0)
     high = lax.broadcasted_iota(jnp.int32, (LANES, BUCKETS // LOW), 1)
     spread = jnp.where(bucket // LOW == high, 1.0, 0.0)
-    spread = dot(spread, sums, NN, **exact)
+    spread = dot(spread.astype(BF), sums.astype(BF), NN)
     bucket = lax.broadcasted_iota(jnp.int32, (LANES, wide), 0)
     column = lax.broadcasted_iota(jnp.int32, (LANES, wide), 1)
     spread = jnp.where(bucket % LOW == column // (heads * GROUP), spread, 0.0)
     head = lax.broadcasted_iota(jnp.int32, (8, wide), 0)
     column = lax.broadcasted_iota(jnp.int32, (8, wide), 1)
     of_head = jnp.where(column // GROUP % heads == head, 1.0, 0.0)
-    by_head = dot(of_head, spread, NT, **exact)
+    by_head = dot(of_head.astype(BF), spread.astype(BF), NT)
     for n in range(dp):
         moved = by_head if n == 0 else pltpu.roll(by_head, LANES - n * BR, 1)
         r.part_m[n // comm.Y, n % comm.Y] = moved
@@ -627,7 +638,8 @@
     for b in range(NB):
         rows = rows_of(2 * b + c, half)
         x = r.x[rows, :].astype(F32)
-        r.s_ig[b] = r.dmid[b] + norm_back(h_in[b].finish(), x, gain_attn)
+        total = r.dmid[b] + norm_back(h_in[b].finish(), x, gain_attn)
+        r.s_ig[b] = total.astype(BF)
         ref = r.input_grad.at[rows]
         comm.send(r.s_ig.at[b], ref, partner, p_ig[b])
         stores.append(local(r.s_ig.at[b], ref))
@@ -654,7 +666,9 @@
         total = jnp.zeros((8, R), F32)
         for weight, grad in pairs:
             product = weight.astype(F32) * grad
-            total = total + dot(jnp.ones((8, product.shape[1]), F32), product, NT, **exact)
+            total = total + dot(
+                jnp.ones((8, product.shape[1]), F32), product, NT, precision=lax.Precision.HIGHEST
+            )
         return total[0:1] / gain.astype(BF).astype(F32)
 
     r.norm[t] = jnp.zeros(r.norm.shape[1:], F32)
@@ -689,21 +703,37 @@
         store.wait()
 
 
-def hand_over(*refs):
-    sems = refs[-1]
-    count = (len(refs) - 1) // 3
-    before, after, held = refs[:count], refs[count : 2 * count], refs[2 * count : 3 * count]
-    loads = [
-        pltpu.make_async_copy(a, b, sems.at[2 * n]) for n, (a, b) in enumerate(zip(before, held))
-    ]
-    stores = [
-        pltpu.make_async_copy(a, b, sems.at[2 * n + 1]) for n, (a, b) in enumerate(zip(held, after))
-    ]
-    for load in loads:
-        load.start()
-    for load, store in zip(loads, stores):
-        load.wait()
-        store.start()
+def hand_over(names, pieces, *refs):
+    count = len(names)
+    before, after, held = [dict(zip(names, refs[n * count : (n + 1) * count])) for n in range(3)]
+    wide, sems = refs[3 * count :]
+    sem_at = iter(range(4 * (count + 2 * pieces)))
+
+    def parts(name):
+        rows = before[name].shape[0]
+        step = rows // pieces if name in ("block_out", "input_grad") else rows
+        return [slice(k, k + step) for k in range(0, rows, step)]
+
+    jobs = []
+    order = ["input_grad", "block_out"] + [n for n in names if n not in ("input_grad", "block_out")]
+    for name in order:
+        for rows in parts(name):
+            copy = pltpu.make_async_copy(
+                before[name].at[rows], held[name].at[rows], sems.at[next(sem_at)]
+            )
+            copy.start()
+            jobs.append((name, rows, copy))
+    stores = []
+    for name, rows, copy in jobs:
+        copy.wait()
+        source = held[name]
+        if name == "input_grad":
+            wide[rows, :] = source[rows, :].astype(F32)
+            source = wide
+        stores.append(
+            pltpu.make_async_copy(source.at[rows], after[name].at[rows], sems.at[next(sem_at)])
+        )
+        stores[-1].start()
     for store in stores:
         store.wait()
 
@@ -752,7 +782,7 @@
     )
     outputs = dict(
         block_out=S((T, D), BF),
-        input_grad=S((T, D), F32),
+        input_grad=S((T, D), BF),
         o_q=S((R, I), F32),
         o_k=S((R, I), F32),
         o_v=S((R, I), F32),
@@ -816,7 +846,7 @@
         ds=V((heads, T, T), BF),
         bias_sum=V((BUCKETS // LOW * GROUP, LOW * heads * GROUP), F32),
         s_bo=V((NB, half, D), BF),
-        s_ig=V((NB, half, D), F32),
+        s_ig=V((NB, half, D), BF),
         norm=V((tensor, 8, LANES), F32),
         s_m=V((heads, BR), F32),
         s_na=V((1, R), F32),
@@ -850,13 +880,15 @@
         ),
         name="layer",
     )(*inputs.values())
+    final = {**outputs, "input_grad": S((T, D), F32)}
+    pieces = 4
     made = pl.pallas_call(
-        hand_over,
-        out_shape=list(outputs.values()),
+        functools.partial(hand_over, list(outputs), pieces),
+        out_shape=list(final.values()),
         in_specs=[pl.BlockSpec(memory_space=pl.ANY)] * len(outputs),
         out_specs=[pl.BlockSpec(memory_space=pl.ANY)] * len(outputs),
         scratch_shapes=[V(o.shape, o.dtype) for o in outputs.values()]
-        + [pltpu.SemaphoreType.DMA((2 * len(outputs),))],
+        + [V((T, D), F32), pltpu.SemaphoreType.DMA((4 * (len(outputs) + 2 * pieces),))],
         name="hand_over",
     )(*made)
     out = dict(zip(outputs, made))

time: 83.9 us -> 83.3 us (level)
  no operation moved by 1% of the time
where the time goes in v4:
time: 83.3 us; the launch traced here: 83.2 us
  Pallas kernels  82.3 us (99%)
  between operations  0.84 us (1%)
    pallas_call x1, Pallas kernels, per_device(): pl.pallas_call(functools.partial(layer_kernel, sizes, heads, names), out_...  78.8 us
    pallas_call x1, Pallas kernels, per_device(): pl.pallas_call(functools.partial(hand_over, list(outputs), pieces), out_s...  3.53 us

profile of v4, /device:TPU:0, one launch (start us, length us, event | category | flops | bytes accessed | tf_op | source)
XLA Modules:
  0.0 83.2 jit_solution(6994385857295689231)
XLA Ops:
  0.6 78.8 %layer.1 = (bf16[1024,512]{1,0:T(8,128)(2,1)}, bf16[1024,512]{1,0:T(8,128)(2,1)}, f32[64,128]{1,0:T(8,128)}, f32[64,128]{1,0:T(8,128)}, f32[64,128]{1,0:T(8,128)...) custom-call(bf16[1024,512]{1,0:T(8,128)(2,1)} %refs_0_.1, ...), custom_call_target="tpu_custom_call" | custom-call | tf_op jit(solution)/shard_map/layer/pallas_call | solution.py:872
  79.5 3.5 %hand_over.1 = (bf16[1024,512]{1,0:T(8,128)(2,1)}, f32[1024,512]{1,0:T(8,128)}, f32[64,128]{1,0:T(8,128)}, f32[64,128]{1,0:T(8,128)}, f32[64,128]{1,0:T(8,128)},...) custom-call(bf16[1024,512]{1,0:T(8,128)(2,1)} %get-tuple-element.36., ...), custom_call_target="tpu_custom_call" | custom-call | tf_op jit(solution)/shard_map/hand_over/pallas_call | solution.py:885

commit v5 on v4

--- a/solution.py
+++ b/solution.py
@@ -547,8 +547,6 @@
                 more_k, more_v = r.dk[h] + more_k, r.dv[h] + more_v
             r.dk[h], r.dv[h] = more_k, more_v
         r.da[rows, 0:I] = jnp.concatenate(made, axis=1)
-        more = dot(r.dmb[rows, :], r.o_all[t, rows, :], TN)
-        r.go[...] = more if b == 0 else r.go[...] + more
 
     for b in range(NB):
         made = feed(b)
@@ -565,7 +563,7 @@
     for b in range(1, NB):
         to_middle(b)
         back(b - 1)
-        if b == 2:
+        if b == 3:
             sc["d"].middle()
     h_out[0].middle()
     back(NB - 1)
@@ -580,10 +578,9 @@
             h_in[b - 1].middle()
     scatter_grad("a", dot(r.n1[...], r.da[...], TN))
     h_in[NB - 1].middle()
-    scatter_grad("o", r.go[...])
+    scatter_grad("o", dot(r.dmb[...], r.o_all[t], TN))
     sc["g"].middle()
-    for b in range(1, NB):
-        h_out[b].middle()
+    h_out[1].middle()
 
     def bias_rows(i, carry):
         former, latter = [], []
@@ -608,8 +605,10 @@
     count = T // (GROUP * GROUPS)
     sums = lax.fori_loop(0, count // 2, bias_rows, jnp.zeros(r.bias_sum.shape, F32))
     r.bias_sum[...] = sums
+    for b in range(2, NB):
+        h_out[b].middle()
+    sc["u"].middle()
     sc["a"].middle()
-    sc["u"].middle()
     sums = r.bias_sum[...]
     sums = lax.fori_loop(count // 2, count, bias_rows, sums)
     tall, wide = r.bias_sum.shape
@@ -842,7 +841,6 @@
         dk=V((heads, T, HD), F32),
         dv=V((heads, T, HD), F32),
         da=V((T, 3 * I), BF),
-        go=V((D, I), F32),
         ds=V((heads, T, T), BF),
         bias_sum=V((BUCKETS // LOW * GROUP, LOW * heads * GROUP), F32),
         s_bo=V((NB, half, D), BF),

time: 83.3 us -> 83.3 us (level)
  no operation moved by 1% of the time
where the time goes in v5:
time: 83.3 us; the launch traced here: 83.1 us
  Pallas kernels  82.3 us (99%)
  between operations  0.84 us (1%)
    pallas_call x1, Pallas kernels, per_device(): pl.pallas_call(functools.partial(layer_kernel, sizes, heads, names), out_...  78.8 us
    pallas_call x1, Pallas kernels, per_device(): pl.pallas_call(functools.partial(hand_over, list(outputs), pieces), out_s...  3.53 us

profile of v5, /device:TPU:0, one launch (start us, length us, event | category | flops | bytes accessed | tf_op | source)
XLA Modules:
  0.0 83.1 jit_solution(7823420072123527289)
XLA Ops:
  0.6 78.8 %layer.1 = (bf16[1024,512]{1,0:T(8,128)(2,1)}, bf16[1024,512]{1,0:T(8,128)(2,1)}, f32[64,128]{1,0:T(8,128)}, f32[64,128]{1,0:T(8,128)}, f32[64,128]{1,0:T(8,128)...) custom-call(bf16[1024,512]{1,0:T(8,128)(2,1)} %refs_0_.1, ...), custom_call_target="tpu_custom_call" | custom-call | tf_op jit(solution)/shard_map/layer/pallas_call | solution.py:870
  79.4 3.5 %hand_over.1 = (bf16[1024,512]{1,0:T(8,128)(2,1)}, f32[1024,512]{1,0:T(8,128)}, f32[64,128]{1,0:T(8,128)}, f32[64,128]{1,0:T(8,128)}, f32[64,128]{1,0:T(8,128)},...) custom-call(bf16[1024,512]{1,0:T(8,128)(2,1)} %get-tuple-element.36., ...), custom_call_target="tpu_custom_call" | custom-call | tf_op jit(solution)/shard_map/hand_over/pallas_call | solution.py:883
